TPU v7x, 32 devices: a whole 2x2x4 slice. The times are simulated.
32 devices in a mesh: fsdp: 4 (over z), expert: 8 (over y, x, core).
Axes of the slice: x: 2, y: 2, z: 4, core: 2. Of those that a mesh axis runs over, the one named last changes fastest.
Arguments:
- residual_in: bfloat16 [4, 1024, 1536], P('fsdp', 'expert'), may hold values from -30 to 30
- cotangent: bfloat16 [4, 1024, 1536], P('fsdp', 'expert'), may hold values from -30 to 30
- gain_attn: bfloat16 [1536], P('fsdp'), may hold values from 0.5 to 1.5
- w_query: bfloat16 [1536, 1536], P('fsdp'), may hold values from -0.5 to 0.5
- w_key: bfloat16 [1536, 512], P('fsdp'), may hold values from -0.5 to 0.5
- w_value: bfloat16 [1536, 512], P('fsdp'), may hold values from -0.625 to 0.625
- w_out: bfloat16 [1536, 1536], P(None, 'fsdp'), may hold values from -1.5 to 1.5
- gain_ffn: bfloat16 [1536], P('fsdp'), may hold values from 0.5 to 1.5
- w_router: bfloat16 [1536, 24], P('fsdp'), may hold values from -0.078125 to 0.078125
- w_gate: bfloat16 [24, 1536, 512], P('expert'), may hold values from -0.15625 to 0.15625
- w_up: bfloat16 [24, 1536, 512], P('expert'), may hold values from -0.15625 to 0.15625
- w_down: bfloat16 [24, 512, 1536], P('expert'), may hold values from -4 to 4
- route_ids: int32 [4, 1024, 8], P('fsdp', 'expert'), may hold values from 0 to 23, all different within a row; in each aligned block of 128 rows (0 to 127, 128 to 255, ..., all dimensions but the last counted through in order) at most 64 rows name the same one
Outputs:
- output: bfloat16 [4, 1024, 1536], P('fsdp', 'expert')
- input_grad: bfloat16 [4, 1024, 1536], P('fsdp', 'expert')
- grad_gain_attn: float32 [1536], P('fsdp')
- grad_query: float32 [1536, 1536], P('fsdp')
- grad_key: float32 [1536, 512], P('fsdp')
- grad_value: float32 [1536, 512], P('fsdp')
- grad_out_proj: float32 [1536, 1536], P(None, 'fsdp')
- grad_gain_ffn: float32 [1536], P('fsdp')
- grad_router: float32 [1536, 24], P('fsdp')
- grad_gate: float32 [24, 1536, 512], P('expert', 'fsdp')
- grad_up: float32 [24, 1536, 512], P('expert', 'fsdp')
- grad_down: float32 [24, 512, 1536], P('expert', None, 'fsdp')
- residual_rms: float32 [5], replicated
Inputs may be any that keep to these rules, and one draw needn't show every extreme that they name: `route_ids`: each token names 8 different experts; within the 128 tokens of one device (aligned blocks of the flattened sequences) no expert is named more than 64 times, a bound that some block reaches.
All inputs are finite; a program needn't handle non-finite values.
Results may differ from a plain program's by a relative error of at most 0.024.
Values may be sent and summed in bfloat16 or wider, within the bound.
A program may use at most 256 MiB of HBM per device.

v0:
```python
import functools

import jax
import jax.numpy as jnp
from jax import lax
from jax.experimental import pallas as pl
from jax.experimental.pallas import tpu as pltpu
from jax.sharding import PartitionSpec as P

HEAD_DIM = 64
BLOCK = 256

EPSILON = 1e-06
RESIDUAL_SCALE = 0.22
ATTENTION_SCALE = 0.015625
ROPE_BASE = 10000.0
HIGHEST = lax.Precision.HIGHEST
MESH = pl.DeviceIdType.MESH
VMEM_LIMIT = 63_000_000
F32 = jnp.float32
BF16 = jnp.bfloat16
LANES = 128


def plane_neighbours():
    me = lax.axis_index("expert")
    core = lax.rem(me, 2)
    x_bit = lax.rem(me // 2, 2)
    y_bit = me // 4
    sibling = me + 1 - 2 * core
    x_peer = me + 2 - 4 * x_bit
    y_peer = me + 4 - 8 * y_bit
    diagonal = x_peer + 4 - 8 * y_bit
    return me, core, x_bit, y_bit, sibling, x_peer, y_peer, diagonal


def greet(axis, peers):
    barrier = pltpu.get_barrier_semaphore()
    for peer in peers:
        pl.semaphore_signal(barrier, inc=1, device_id={axis: peer}, device_id_type=MESH)
    pl.semaphore_wait(barrier, len(peers))


def gather_kernel(count, *refs):
    ins, outs = refs[:count], refs[count : 2 * count]
    own_sem, send_sem, recv_sem = refs[2 * count :]
    me, _, _, _, sibling, x_peer, y_peer, diagonal = plane_neighbours()
    greet("expert", (sibling, x_peer, y_peer))

    def remote(k, slot, source, target, peer):
        return pltpu.make_async_remote_copy(
            src_ref=source,
            dst_ref=target,
            send_sem=send_sem.at[k, slot],
            recv_sem=recv_sem.at[k, slot],
            device_id={"expert": peer},
            device_id_type=MESH,
        )

    plans = []
    for k in range(count):
        half = ins[k].shape[0] // 2
        parts = (pl.ds(0, half), pl.ds(half, half))
        out = outs[k]
        own = pltpu.make_async_copy(ins[k], out.at[me], own_sem.at[k])
        copies = [remote(k, 0, ins[k], out.at[me], sibling)]
        for h in range(2):
            copies.append(remote(k, 1 + h, ins[k].at[parts[h]], out.at[me, parts[h]], x_peer))
        for h in range(2):
            copies.append(remote(k, 3 + h, ins[k].at[parts[h]], out.at[me, parts[h]], y_peer))

        def forward(slot, block, h, peer):
            return remote(k, slot, out.at[block, parts[h]], out.at[block, parts[h]], peer)

        copies.append(forward(5, y_peer, 0, x_peer))
        copies.append(forward(6, x_peer, 1, y_peer))
        for h in range(2):
            copies.append(forward(7 + h, x_peer, h, sibling))
        for h in range(2):
            copies.append(forward(9 + h, y_peer, h, sibling))
        for h in range(2):
            copies.append(forward(11 + h, diagonal, h, sibling))
        plans.append((own, copies))
    for own, copies in plans:
        for slot in (3, 2, 1, 4, 0):
            copies[slot].start()
        own.start()
    for own, copies in plans:
        copies[3].wait_recv()
        copies[5].start()
        copies[2].wait_recv()
        copies[6].start()
        copies[9].start()
        copies[8].start()
        copies[1].wait_recv()
        copies[7].start()
        copies[4].wait_recv()
        copies[10].start()
    for own, copies in plans:
        copies[5].wait_recv()
        copies[11].start()
        copies[6].wait_recv()
        copies[12].start()
    for own, copies in plans:
        for slot in (0, 7, 8, 9, 10, 11, 12):
            copies[slot].wait_recv()
        for copy in copies:
            copy.wait_send()
        own.wait()


def plane_gather(arrays, collective_id):
    if lax.axis_size("expert") != 8:
        return [lax.all_gather(array, "expert", axis=0) for array in arrays]
    count = len(arrays)
    size = sum(array.size * array.dtype.itemsize for array in arrays)
    return pl.pallas_call(
        functools.partial(gather_kernel, count),
        out_shape=[jax.ShapeDtypeStruct((8,) + array.shape, array.dtype) for array in arrays],
        in_specs=[pl.BlockSpec(memory_space=pltpu.VMEM)] * count,
        out_specs=[pl.BlockSpec(memory_space=pl.ANY)] * count,
        scratch_shapes=[
            pltpu.SemaphoreType.DMA((count,)),
            pltpu.SemaphoreType.DMA((count, 13)),
            pltpu.SemaphoreType.DMA((count, 13)),
        ],
        compiler_params=pltpu.CompilerParams(
            collective_id=collective_id, has_side_effects=True, vmem_limit_bytes=VMEM_LIMIT
        ),
        cost_estimate=pl.CostEstimate(flops=0, bytes_accessed=16 * size, transcendentals=0),
        name="plane_gather",
    )(*arrays)


def scatter_kernel(count, *refs):
    ins, outs = refs[:count], refs[count : 2 * count]
    scratch = refs[2 * count : 2 * count + 6 * count]
    send_sem, recv_sem = refs[8 * count :]
    me, core, x_bit, y_bit, sibling, x_peer, y_peer, diagonal = plane_neighbours()
    greet("expert", (sibling, x_peer, y_peer))
    chip = me // 2
    chip_x, chip_y, chip_d = x_peer // 2, y_peer // 2, diagonal // 2
    order = (chip_d, chip_x, chip_y, chip)

    def remote(k, slot, source, target, peer):
        return pltpu.make_async_remote_copy(
            src_ref=source,
            dst_ref=target,
            send_sem=send_sem.at[k, slot],
            recv_sem=recv_sem.at[k, slot],
            device_id={"expert": peer},
            device_id_type=MESH,
        )

    stage0 = []
    for k in range(count):
        pair = scratch[6 * k]
        copies = [
            remote(k, i, ins[k].at[2 * order[i] + 1 - core], pair.at[i], sibling) for i in range(4)
        ]
        stage0.append(copies)
        for copy in copies:
            copy.start()
    later = []
    for k in range(count):
        pair, sums, first_x, first_y, second_x, second_y = scratch[6 * k : 6 * k + 6]
        rows = ins[k].shape[1]
        half = rows // 2
        parts = (pl.ds(0, half), pl.ds(half, half))
        dtype = ins[k].dtype

        def join(i):
            stage0[k][i].wait_recv()
            sums[i] = (ins[k][2 * order[i] + core].astype(F32) + pair[i].astype(F32)).astype(dtype)

        join(0)
        copies = [
            remote(k, 4, sums.at[0, parts[0]], first_x.at[1], x_peer),
            remote(k, 5, sums.at[0, parts[1]], first_y.at[1], y_peer),
        ]
        for copy in copies:
            copy.start()
        join(1)
        copies.append(remote(k, 6, sums.at[1, parts[0]], first_x.at[0], x_peer))
        copies[-1].start()
        join(2)
        copies.append(remote(k, 7, sums.at[2, parts[1]], first_y.at[0], y_peer))
        copies[-1].start()
        join(3)
        later.append(copies)
    for k in range(count):
        pair, sums, first_x, first_y, second_x, second_y = scratch[6 * k : 6 * k + 6]
        half = ins[k].shape[1] // 2
        parts = (pl.ds(0, half), pl.ds(half, half))
        dtype = ins[k].dtype
        copies = later[k]
        copies[0].wait_recv()
        pair[0, parts[0]] = (
            sums[2, parts[0]].astype(F32) + first_x[1].astype(F32)
        ).astype(dtype)
        copies.append(remote(k, 8, pair.at[0, parts[0]], second_y, y_peer))
        copies[-1].start()
        copies[1].wait_recv()
        pair[0, parts[1]] = (
            sums[1, parts[1]].astype(F32) + first_y[1].astype(F32)
        ).astype(dtype)
        copies.append(remote(k, 9, pair.at[0, parts[1]], second_x, x_peer))
        copies[-1].start()
    for k in range(count):
        pair, sums, first_x, first_y, second_x, second_y = scratch[6 * k : 6 * k + 6]
        half = ins[k].shape[1] // 2
        parts = (pl.ds(0, half), pl.ds(half, half))
        copies = later[k]
        copies[2].wait_recv()
        copies[4].wait_recv()
        outs[k][parts[0]] = (
            sums[3, parts[0]].astype(F32) + first_x[0].astype(F32) + second_y[...].astype(F32)
        )
        copies[3].wait_recv()
        copies[5].wait_recv()
        outs[k][parts[1]] = (
            sums[3, parts[1]].astype(F32) + first_y[0].astype(F32) + second_x[...].astype(F32)
        )
        for copy in stage0[k] + copies:
            copy.wait_send()


def plane_scatter(arrays, collective_id):
    if lax.axis_size("expert") != 8:
        return [
            lax.psum_scatter(array, "expert", scatter_dimension=0, tiled=False).astype(F32)
            for array in arrays
        ]
    count = len(arrays)
    scratch = []
    for array in arrays:
        _, rows, columns = array.shape
        half = rows // 2
        for shape in (
            (4, rows, columns),
            (4, rows, columns),
            (2, half, columns),
            (2, half, columns),
            (half, columns),
            (half, columns),
        ):
            scratch.append(pltpu.VMEM(shape, array.dtype))
    size = sum(array.size * array.dtype.itemsize for array in arrays)
    return pl.pallas_call(
        functools.partial(scatter_kernel, count),
        out_shape=[jax.ShapeDtypeStruct(array.shape[1:], F32) for array in arrays],
        in_specs=[pl.BlockSpec(memory_space=pltpu.VMEM)] * count,
        out_specs=[pl.BlockSpec(memory_space=pltpu.VMEM)] * count,
        scratch_shapes=scratch
        + [pltpu.SemaphoreType.DMA((count, 10)), pltpu.SemaphoreType.DMA((count, 10))],
        compiler_params=pltpu.CompilerParams(
            collective_id=collective_id, has_side_effects=True, vmem_limit_bytes=VMEM_LIMIT
        ),
        cost_estimate=pl.CostEstimate(flops=0, bytes_accessed=3 * size, transcendentals=0),
        name="plane_scatter",
    )(*arrays)


def push(source, target, send_sem, recv_sem, axis, peer):
    return pltpu.make_async_remote_copy(
        src_ref=source,
        dst_ref=target,
        send_sem=send_sem,
        recv_sem=recv_sem,
        device_id={axis: peer},
        device_id_type=MESH,
    )


def meet(plane, line, size, with_line):
    barrier = pltpu.get_barrier_semaphore()
    me, _, _, _, sibling, x_peer, y_peer, _ = plane
    for peer in (sibling, x_peer, y_peer):
        pl.semaphore_signal(barrier, inc=1, device_id={"expert": peer}, device_id_type=MESH)
    pl.semaphore_signal(
        barrier, inc=1, device_id={"fsdp": pair_of(line)}, device_id_type=MESH
    )
    if not with_line:
        pl.semaphore_signal(
            barrier, inc=1, device_id={"fsdp": beside(line)}, device_id_type=MESH
        )
        pl.semaphore_wait(barrier, 5)
        return

    @pl.when(line > 0)
    def _():
        pl.semaphore_signal(barrier, inc=1, device_id={"fsdp": line - 1}, device_id_type=MESH)

    @pl.when(line < size - 1)
    def _():
        pl.semaphore_signal(barrier, inc=1, device_id={"fsdp": line + 1}, device_id_type=MESH)

    @pl.when((line > 0) & (line < size - 1))
    def _():
        pl.semaphore_wait(barrier, 6)

    @pl.when((line == 0) | (line == size - 1))
    def _():
        pl.semaphore_wait(barrier, 5)


def pair_of(line):
    return line + 2 - 4 * (line // 2)


def beside(line):
    return line + 1 - 2 * lax.rem(line, 2)


def norm_back(grad_normed, normed, inverse):
    return inverse * (grad_normed - normed * jnp.mean(grad_normed * normed, axis=-1, keepdims=True))


class Gather:
    def __init__(self, plane, k, source, out, base, own_sem, send_sem, recv_sem):
        me, _, _, _, sibling, x_peer, y_peer, diagonal = plane
        half = source.shape[0] // 2
        parts = (pl.ds(0, half), pl.ds(half, half))

        def copy(slot, src, dst, peer):
            return push(src, dst, send_sem.at[k, slot], recv_sem.at[k, slot], "expert", peer)

        def forward(slot, block, h, peer):
            ref = out.at[base + block, parts[h]]
            return copy(slot, ref, ref, peer)

        self.own = pltpu.make_async_copy(source, out.at[base + me], own_sem.at[k])
        copies = [copy(0, source, out.at[base + me], sibling)]
        for slot, peer in ((1, x_peer), (3, y_peer)):
            for h in range(2):
                copies.append(
                    copy(slot + h, source.at[parts[h]], out.at[base + me, parts[h]], peer)
                )
        copies.append(forward(5, y_peer, 0, x_peer))
        copies.append(forward(6, x_peer, 1, y_peer))
        for slot, block in ((7, x_peer), (9, y_peer), (11, diagonal)):
            for h in range(2):
                copies.append(forward(slot + h, block, h, sibling))
        self.copies = copies

    def begin(self):
        for slot in (3, 2, 1, 4, 0):
            self.copies[slot].start()
        self.own.start()

    def relay(self):
        copies = self.copies
        for landed, onward in ((3, (5, 9)), (2, (6, 8)), (1, (7,)), (4, (10,))):
            copies[landed].wait_recv()
            for slot in onward:
                copies[slot].start()

    def relay_diagonal(self):
        for landed, onward in ((5, 11), (6, 12)):
            self.copies[landed].wait_recv()
            self.copies[onward].start()

    def finish(self):
        for slot in (0, 7, 8, 9, 10, 11, 12):
            self.copies[slot].wait_recv()
        for copy in self.copies:
            copy.wait_send()
        self.own.wait()


def gather_sems(count):
    return [
        pltpu.SemaphoreType.DMA((count,)),
        pltpu.SemaphoreType.DMA((count, 13)),
        pltpu.SemaphoreType.DMA((count, 13)),
    ]


class Scatter:
    def __init__(self, plane, k, source, base, scratch, send_sem, recv_sem):
        me, core, _, _, sibling, x_peer, y_peer, diagonal = plane
        self.source, self.base, self.core = source, base, core
        self.pair, self.first_x, self.first_y, self.second_x, self.second_y = scratch[:5]
        self.order = (diagonal // 2, x_peer // 2, y_peer // 2, me // 2)
        self.sums = [
            scratch[5].at[i] if len(scratch) > 5 else source.at[base + 2 * self.order[i] + core]
            for i in range(4)
        ]
        self.dtype = source.dtype
        half = source.shape[1] // 2
        self.parts = parts = (pl.ds(0, half), pl.ds(half, half))

        def copy(slot, src, dst, peer):
            return push(src, dst, send_sem.at[k, slot], recv_sem.at[k, slot], "expert", peer)

        self.stage0 = [
            copy(i, source.at[base + 2 * self.order[i] + 1 - core], self.pair.at[i], sibling)
            for i in range(4)
        ]
        self.stage1 = [
            copy(4, self.sums[0].at[parts[0]], self.first_x.at[1], x_peer),
            copy(5, self.sums[0].at[parts[1]], self.first_y.at[1], y_peer),
            copy(6, self.sums[1].at[parts[0]], self.first_x.at[0], x_peer),
            copy(7, self.sums[2].at[parts[1]], self.first_y.at[0], y_peer),
        ]
        self.stage2 = [
            copy(8, self.pair.at[0, parts[0]], self.second_y, y_peer),
            copy(9, self.pair.at[0, parts[1]], self.second_x, x_peer),
        ]

    def begin(self):
        for copy in self.stage0:
            copy.start()

    def join(self, i):
        self.stage0[i].wait_recv()
        mine = self.source[self.base + 2 * self.order[i] + self.core]
        self.sums[i][...] = (mine.astype(F32) + self.pair[i].astype(F32)).astype(self.dtype)

    def first(self):
        self.join(0)
        self.stage1[0].start()
        self.stage1[1].start()
        self.join(1)
        self.stage1[2].start()
        self.join(2)
        self.stage1[3].start()
        self.join(3)

    def second(self):
        for h, block, landed in ((0, 2, self.first_x), (1, 1, self.first_y)):
            self.stage1[h].wait_recv()
            rows = self.parts[h]
            self.pair[0, rows] = (
                self.sums[block][rows].astype(F32) + landed[1].astype(F32)
            ).astype(self.dtype)
            self.stage2[h].start()

    def total(self, h):
        self.stage1[2 + h].wait_recv()
        self.stage2[h].wait_recv()
        near, far = ((self.first_x, self.second_y), (self.first_y, self.second_x))[h]
        return (
            self.sums[3][self.parts[h]].astype(F32)
            + near[0].astype(F32)
            + far[...].astype(F32)
        )

    def finish(self):
        for copy in self.stage0 + self.stage1 + self.stage2:
            copy.wait_send()


def scatter_scratch(rows, columns, dtype, in_place=False):
    half = rows // 2
    shapes = [
        (4, rows, columns),
        (2, half, columns),
        (2, half, columns),
        (half, columns),
        (half, columns),
        (4, rows, columns),
    ]
    return [pltpu.VMEM(shape, dtype) for shape in shapes[: 5 if in_place else 6]]


def scatter_sems(count):
    return [pltpu.SemaphoreType.DMA((count, 10)), pltpu.SemaphoreType.DMA((count, 10))]


class LineGather:
    def __init__(self, line, size, k, source, out, axis, own_sem, send_sem, recv_sem):
        self.line, self.size, self.k, self.source, self.out = line, size, k, source, out
        self.axis, self.send_sem, self.recv_sem = axis, send_sem, recv_sem
        self.own = pltpu.make_async_copy(source, self.place(line), own_sem.at[k])

    def place(self, owner):
        extent = self.source.shape[self.axis]
        span = pl.ds(pl.multiple_of(owner * extent, extent), extent)
        return self.out.at[span] if self.axis == 0 else self.out.at[:, span]

    def hop(self, side, step, owner, source=None):
        target = self.place(owner)
        return push(
            target if source is None else source,
            target,
            self.send_sem.at[self.k, side, step],
            self.recv_sem.at[self.k, side, step],
            "fsdp",
            self.line + 1 - 2 * side,
        )

    def begin(self):
        for side, there in ((0, self.line < self.size - 1), (1, self.line > 0)):

            @pl.when(there)
            def _():
                self.hop(side, 0, self.line, self.source).start()

        self.own.start()

    def step(self, step):
        line, last = self.line, self.size - 1
        for side, owner in ((0, line - 1 - step), (1, line + 1 + step)):

            @pl.when((owner >= 0) & (owner <= last))
            def _():
                self.hop(side, step, owner).wait_recv()

                @pl.when((line < last) if side == 0 else (line > 0))
                def _():
                    self.hop(side, step + 1, owner).start()

    def finish(self):
        line, last = self.line, self.size - 1
        self.own.wait()
        for step in range(self.size - 1):
            for side, owner, there in ((0, line - step, line < last), (1, line + step, line > 0)):

                @pl.when(there & (owner >= 0) & (owner <= last))
                def _():
                    self.hop(side, step, owner).wait_send()


def line_gather_sems(count, size):
    return [
        pltpu.SemaphoreType.DMA((count,)),
        pltpu.SemaphoreType.DMA((count, 2, size)),
        pltpu.SemaphoreType.DMA((count, 2, size)),
    ]


class LineScatter:
    def __init__(self, line, size, k, source, sums, landed, send_sem, recv_sem):
        self.line, self.size, self.k = line, size, k
        self.source, self.sums, self.landed = source, sums, landed
        self.send_sem, self.recv_sem = send_sem, recv_sem

    def hop(self, side, owner):
        return push(
            self.sums.at[side, owner],
            self.landed.at[side, owner],
            self.send_sem.at[self.k, side, owner],
            self.recv_sem.at[self.k, side, owner],
            "fsdp",
            self.line + 1 - 2 * side,
        )

    def begin(self):
        last = self.size - 1
        for far in range(last):
            for side, owner, end in ((0, last - far, 0), (1, far, last)):

                @pl.when(self.line == end)
                def _():
                    self.sums[side, owner] = self.source[owner]
                    self.hop(side, owner).start()

    def pass_on(self, side, owner):
        self.hop(side, owner).wait_recv()
        self.sums[side, owner] = (
            self.source[owner].astype(F32) + self.landed[side, owner].astype(F32)
        ).astype(self.source.dtype)
        self.hop(side, owner).start()

    def step(self, far):
        line, last = self.line, self.size - 1

        @pl.when((line < last - far) & (line > 0))
        def _():
            self.pass_on(0, last - far)

        @pl.when((line > far) & (line < last))
        def _():
            self.pass_on(1, far)

    def total(self):
        line, last = self.line, self.size - 1
        for side, there, beyond in ((0, line > 0, line == 0), (1, line < last, line == last)):

            @pl.when(there)
            def _():
                self.hop(side, line).wait_recv()

            @pl.when(beyond)
            def _():
                self.landed[side, line] = jnp.zeros(self.source.shape[1:], self.source.dtype)

        return (
            self.source[line].astype(F32)
            + self.landed[0, line].astype(F32)
            + self.landed[1, line].astype(F32)
        )

    def finish(self):
        for owner in range(self.size):

            @pl.when(self.line < owner)
            def _():
                self.hop(0, owner).wait_send()

            @pl.when(self.line > owner)
            def _():
                self.hop(1, owner).wait_send()


def line_scatter_sems(count, size):
    return [
        pltpu.SemaphoreType.DMA((count, 2, size)),
        pltpu.SemaphoreType.DMA((count, 2, size)),
    ]


def in_vmem(count):
    return [pl.BlockSpec(memory_space=pltpu.VMEM)] * count


def anywhere(count):
    return [pl.BlockSpec(memory_space=pl.ANY)] * count


def talk_params(collective_id):
    return pltpu.CompilerParams(
        collective_id=collective_id, has_side_effects=True, vmem_limit_bytes=VMEM_LIMIT
    )


def open_kernel(
    size, x_ref, dy_ref, win_ref, wout_ref,
    x_out, dy_out, win_out, wout_out,
    landed, swap_sems, own_sem, send_sem, recv_sem, line_own, line_send, line_recv,
):
    plane, line = plane_neighbours(), lax.axis_index("fsdp")
    meet(plane, line, size, True)
    swap = push(dy_ref, landed, swap_sems.at[0], swap_sems.at[1], "fsdp", pair_of(line))
    sems = (own_sem, send_sem, recv_sem)
    line_sems = (line_own, line_send, line_recv)
    x = Gather(plane, 0, x_ref, x_out, 0, *sems)
    dy = Gather(plane, 1, dy_ref, dy_out, 0, *sems)
    other = Gather(plane, 2, landed, dy_out, 8, *sems)
    win = LineGather(line, size, 0, win_ref, win_out, 0, *line_sems)
    wout = LineGather(line, size, 1, wout_ref, wout_out, 1, *line_sems)
    win.begin()
    x.begin()
    swap.start()
    wout.begin()
    dy.begin()
    x.relay()
    win.step(0)
    x.relay_diagonal()
    wout.step(0)
    win.step(1)
    dy.relay()
    swap.wait_recv()
    other.begin()
    wout.step(1)
    dy.relay_diagonal()
    win.step(2)
    wout.step(2)
    other.relay()
    other.relay_diagonal()
    for part in (x, dy, other, win, wout):
        part.finish()
    swap.wait_send()


def open_transfers(x, dy, w_in_shard, w_out_shard, size, collective_id):
    tokens, model_width = x.shape
    rows, columns = w_in_shard.shape
    out_rows, out_columns = w_out_shard.shape
    return pl.pallas_call(
        functools.partial(open_kernel, size),
        out_shape=[
            jax.ShapeDtypeStruct((8, tokens, model_width), BF16),
            jax.ShapeDtypeStruct((16, tokens, model_width), BF16),
            jax.ShapeDtypeStruct((rows * size, columns), BF16),
            jax.ShapeDtypeStruct((out_rows, out_columns * size), BF16),
        ],
        in_specs=in_vmem(4),
        out_specs=anywhere(4),
        scratch_shapes=[pltpu.VMEM((tokens, model_width), BF16), pltpu.SemaphoreType.DMA((2,))]
        + gather_sems(3)
        + line_gather_sems(2, size),
        compiler_params=talk_params(collective_id),
        cost_estimate=pl.CostEstimate(flops=0, bytes_accessed=120_000_000, transcendentals=0),
        name="open_transfers",
    )(x, dy, w_in_shard, w_out_shard)


def middle_kernel(
    query_width, router_at, part_ref, x_ref, win_ref, wout_ref, chosen_ref,
    b_out, g_out, middle_ref, marked_ref,
    routed, b_landed, g_landed, *rest,
):
    scratch, rest = rest[:6], rest[6:]
    swap_sems, scatter_send, scatter_recv, own_sem, send_sem, recv_sem = rest
    plane, line = plane_neighbours(), lax.axis_index("fsdp")
    meet(plane, line, 4, False)
    scatter = Scatter(plane, 0, part_ref, 0, scratch, scatter_send, scatter_recv)
    scatter.begin()
    scatter.first()
    scatter.second()
    half = x_ref.shape[0] // 2
    gain = wout_ref[query_width + 1 : query_width + 2, :].astype(F32)
    router = win_ref[:, router_at : router_at + LANES]
    for h in range(2):
        rows = pl.ds(h * half, half)
        middle = x_ref[rows].astype(F32) + RESIDUAL_SCALE * scatter.total(h)
        middle_ref[rows] = middle
        inverse = lax.rsqrt(jnp.mean(middle * middle, axis=1, keepdims=True) + EPSILON)
        b = (middle * inverse * gain).astype(BF16)
        routed[rows] = b
        chosen = chosen_ref[rows] > 0.0
        logits = jnp.where(chosen, dot(b, router), -1e30)
        lifted = jnp.where(chosen, jnp.exp(logits - jnp.max(logits, axis=1, keepdims=True)), 0.0)
        gates = lifted / jnp.sum(lifted, axis=1, keepdims=True)
        marked_ref[rows] = jnp.where(chosen, gates, -1.0)
    swap_b = push(routed, b_landed, swap_sems.at[0], swap_sems.at[1], "fsdp", pair_of(line))
    swap_g = push(marked_ref, g_landed, swap_sems.at[2], swap_sems.at[3], "fsdp", pair_of(line))
    swap_b.start()
    swap_g.start()
    sems = (own_sem, send_sem, recv_sem)
    b = Gather(plane, 0, routed, b_out, 0, *sems)
    g = Gather(plane, 1, marked_ref, g_out, 0, *sems)
    b_other = Gather(plane, 2, b_landed, b_out, 8, *sems)
    g_other = Gather(plane, 3, g_landed, g_out, 8, *sems)
    b.begin()
    g.begin()
    b.relay()
    g.relay()
    b.relay_diagonal()
    g.relay_diagonal()
    swap_b.wait_recv()
    swap_g.wait_recv()
    b_other.begin()
    g_other.begin()
    b_other.relay()
    g_other.relay()
    b_other.relay_diagonal()
    g_other.relay_diagonal()
    for item in (b, g, b_other, g_other, scatter):
        item.finish()
    swap_b.wait_send()
    swap_g.wait_send()


def middle_transfers(part, x, w_in, w_out, chosen, query_width, router_at, collective_id):
    tokens, model_width = x.shape
    return pl.pallas_call(
        functools.partial(middle_kernel, query_width, router_at),
        out_shape=[
            jax.ShapeDtypeStruct((16, tokens, model_width), BF16),
            jax.ShapeDtypeStruct((16, tokens, LANES), F32),
            jax.ShapeDtypeStruct((tokens, model_width), F32),
            jax.ShapeDtypeStruct((tokens, LANES), F32),
        ],
        in_specs=in_vmem(5),
        out_specs=anywhere(2) + in_vmem(2),
        scratch_shapes=[
            pltpu.VMEM((tokens, model_width), BF16),
            pltpu.VMEM((tokens, model_width), BF16),
            pltpu.VMEM((tokens, LANES), F32),
        ]
        + scatter_scratch(tokens, model_width, BF16)
        + [pltpu.SemaphoreType.DMA((4,))]
        + scatter_sems(1)
        + gather_sems(4),
        compiler_params=talk_params(collective_id),
        cost_estimate=pl.CostEstimate(flops=0, bytes_accessed=150_000_000, transcendentals=0),
        name="middle_transfers",
    )(part, x, w_in, w_out, chosen)


def close_kernel(
    size, query_width, swaps, da_ref, e_own, e_total, x_ref, middle_ref, grad_ref, gain_two_ref, wout_ref,
    gin_ref, out_low, *rest,
):
    sent, rest = rest[:swaps], rest[swaps:]
    outcome_ref, input_grad_ref, in_out, out_out, gains_out, notes_out, *rest = rest
    came, rest = rest[:swaps], rest[swaps:]
    close_steps(
        size, query_width, sent, came, da_ref, e_own, e_total, x_ref, middle_ref, grad_ref,
        gain_two_ref, wout_ref, gin_ref, out_low,
        outcome_ref, input_grad_ref, in_out, out_out, gains_out, notes_out, *rest,
    )


def close_steps(
    size, query_width, sent, came, da_ref, e_own, e_total, x_ref, middle_ref, grad_ref,
    gain_two_ref, wout_ref, gin_ref, out_low,
    outcome_ref, input_grad_ref, in_out, out_out, gains_out, notes_out,
    e_landed, gains, notes, notes_line, in_low, gain_low, notes_low, *rest,
):
    scratch, rest = rest[:6], rest[6:]
    line_scratch, rest = rest[:4], rest[4:]
    (
        across_sems, swap_sems, scatter_send, scatter_recv, sum_send, sum_recv,
        line_own, line_send, line_recv, own_sem, send_sem, recv_sem,
    ) = rest
    plane, line = plane_neighbours(), lax.axis_index("fsdp")
    meet(plane, line, size, True)
    sums = (scatter_send, scatter_recv)
    da = Scatter(plane, 0, da_ref, 0, scratch[:6], *sums)
    across = [
        push(source, target, across_sems.at[0, i], across_sems.at[1, i], "fsdp", pair_of(line))
        for i, (source, target) in enumerate(zip(sent, came))
    ]
    swap = push(e_total, e_landed, swap_sems.at[0], swap_sems.at[1], "fsdp", pair_of(line))
    gin = LineScatter(line, size, 0, gin_ref, *line_scratch[0:2], sum_send, sum_recv)
    gain = LineScatter(line, size, 1, gains, *line_scratch[2:4], sum_send, sum_recv)
    gathers = (own_sem, send_sem, recv_sem)
    out_all = Gather(plane, 1, out_low, out_out, 0, *gathers)
    half = x_ref.shape[0] // 2
    gin.begin()
    da.begin()
    da.first()
    gin.step(0)
    swap.start()
    da.second()
    gin.step(1)
    gin.step(2)
    for copy in across[:1]:
        copy.start()
    out_all.begin()
    gain_one = wout_ref[query_width : query_width + 1, :].astype(F32)
    grad_gain = jnp.zeros((1, x_ref.shape[1]), F32)
    squares = [jnp.zeros((1, 1), F32)] * 5

    def add_square(i, values):
        squares[i] = squares[i] + jnp.sum(
            jnp.sum(values * values, axis=1, keepdims=True), axis=0, keepdims=True
        )

    for h in range(2):
        rows = pl.ds(h * half, half)
        x = x_ref[rows].astype(F32)
        inverse = lax.rsqrt(jnp.mean(x * x, axis=1, keepdims=True) + EPSILON)
        normed = x * inverse
        grad_a = da.total(h)
        grad_gain += jnp.sum(grad_a * normed, axis=0, keepdims=True)
        grad_middle = grad_ref[rows]
        grad_input = grad_middle + norm_back(grad_a * gain_one, normed, inverse)
        input_grad_ref[rows] = grad_input.astype(BF16)
        add_square(0, x)
        add_square(1, middle_ref[rows])
        add_square(3, grad_middle)
        add_square(4, grad_input)
    width = x_ref.shape[1] // size
    row = lax.broadcasted_iota(jnp.int32, gains.shape[1:], 0)
    for p in range(size):
        columns = slice(p * width, (p + 1) * width)
        gains[p] = jnp.where(
            row == 0, grad_gain[:, columns],
            jnp.where(row == 1, gain_two_ref[0:1, columns], 0.0),
        ).astype(BF16)
    gain.begin()
    for copy in across[1:2]:
        copy.start()
    gain.step(0)
    gain.step(1)
    gain.step(2)
    for copy in across[2:]:
        copy.start()
    out_all.relay()
    swap.wait_recv()
    for h in range(2):
        rows = pl.ds(h * half, half)
        outcome = middle_ref[rows] + e_own[rows] + e_landed[rows].astype(F32)
        outcome_ref[rows] = outcome.astype(BF16)
        add_square(2, outcome)
    row = lax.broadcasted_iota(jnp.int32, notes.shape, 0)
    told = jnp.zeros(notes.shape, F32)
    for i in range(5):
        told = jnp.where(row == i, squares[i], told)
    notes[...] = told
    spread = LineGather(line, size, 0, notes, notes_line, 0, line_own, line_send, line_recv)
    spread.begin()
    in_low[...] = gin.total().astype(BF16)
    in_all = Gather(plane, 0, in_low, in_out, 0, *gathers)
    in_all.begin()
    spread.step(0)
    out_all.relay_diagonal()
    spread.step(1)
    spread.step(2)
    gain_low[...] = gain.total().astype(BF16)
    gain_all = Gather(plane, 2, gain_low, gains_out, 0, *gathers)
    gain_all.begin()
    spread.finish()
    count = notes.shape[0]
    notes_low[...] = (
        notes_line[pl.ds(0, count)] + notes_line[pl.ds(count, count)]
        + notes_line[pl.ds(2 * count, count)] + notes_line[pl.ds(3 * count, count)]
    )
    notes_all = Gather(plane, 3, notes_low, notes_out, 0, *gathers)
    notes_all.begin()
    last = (in_all, gain_all, notes_all)
    for item in last:
        item.relay()
    for item in last:
        item.relay_diagonal()
    for item in last + (out_all, da, gin, gain):
        item.finish()
    swap.wait_send()
    for copy in across:
        copy.wait()


def close_transfers(
    da_part, e_own, e_total, x, middle, grad_middle, gain_two, w_out, grad_in, out_low, sent,
    query_width, collective_id,
):
    tokens, model_width = x.shape
    size, in_rows, in_columns = grad_in.shape
    out_rows, out_columns = out_low.shape
    wide = (tokens, model_width)
    gain_shape, note_shape = (16, out_columns), (16, LANES)
    line_scratch = []
    for shape in (grad_in.shape, (size,) + gain_shape):
        line_scratch += [pltpu.VMEM((2,) + shape, BF16)] * 2
    return pl.pallas_call(
        functools.partial(close_kernel, size, query_width, len(sent)),
        out_shape=[
            jax.ShapeDtypeStruct(wide, BF16),
            jax.ShapeDtypeStruct(wide, BF16),
            jax.ShapeDtypeStruct((8, in_rows, in_columns), BF16),
            jax.ShapeDtypeStruct((8, out_rows, out_columns), BF16),
            jax.ShapeDtypeStruct((8,) + gain_shape, BF16),
            jax.ShapeDtypeStruct((8,) + note_shape, F32),
        ]
        + [jax.ShapeDtypeStruct(array.shape, array.dtype) for array in sent],
        in_specs=in_vmem(10) + anywhere(len(sent)),
        out_specs=in_vmem(2) + anywhere(4 + len(sent)),
        scratch_shapes=[
            pltpu.VMEM(wide, BF16),
            pltpu.VMEM((size,) + gain_shape, BF16),
            pltpu.VMEM(note_shape, F32),
            pltpu.VMEM((size * note_shape[0], LANES), F32),
            pltpu.VMEM((in_rows, in_columns), BF16),
            pltpu.VMEM(gain_shape, BF16),
            pltpu.VMEM(note_shape, F32),
        ]
        + scatter_scratch(*wide, BF16)
        + line_scratch
        + [pltpu.SemaphoreType.DMA((2, len(sent))), pltpu.SemaphoreType.DMA((2,))]
        + scatter_sems(1)
        + line_scatter_sems(2, size)
        + line_gather_sems(1, size)
        + gather_sems(4),
        compiler_params=talk_params(collective_id),
        cost_estimate=pl.CostEstimate(flops=0, bytes_accessed=200_000_000, transcendentals=0),
        name="close_transfers",
    )(da_part, e_own, e_total, x, middle, grad_middle, gain_two, w_out, grad_in, out_low, *sent)


def dot(first, second, contract=(1, 0)):
    return lax.dot_general(
        first, second, (((contract[0],), (contract[1],)), ((), ())), preferred_element_type=F32
    )


def spin(values, cosine, sine):
    width = values.shape[1]
    half = HEAD_DIM // 2
    cosine = jnp.concatenate([cosine] * (width // LANES), axis=1)
    sine = jnp.concatenate([sine] * (width // LANES), axis=1)
    lane = lax.broadcasted_iota(jnp.int32, values.shape, 1)
    lower = lax.rem(lane, HEAD_DIM) < half
    swapped = jnp.where(
        lower, pltpu.roll(values, width - half, 1), pltpu.roll(values, half, 1)
    )
    return values * cosine + swapped * sine


def attend_kernel(
    per_group, x_ref, w_in_ref, w_out_ref, cos_ref, sin_ref,
    part_ref, a_ref, q_ref, k_ref, v_ref, o_ref, lse_ref,
):
    length, model_width = x_ref.shape
    query_width = per_group * HEAD_DIM
    turned = query_width + HEAD_DIM
    gain = w_out_ref[query_width : query_width + 1, :].astype(F32)

    def project(i, carry):
        rows = pl.ds(pl.multiple_of(i * BLOCK, BLOCK), BLOCK)
        x = x_ref[rows, :].astype(F32)
        inverse = lax.rsqrt(jnp.mean(x * x, axis=1, keepdims=True) + EPSILON)
        a = (x * inverse * gain).astype(BF16)
        a_ref[rows, :] = a
        pre = dot(a, w_in_ref[...])
        spun = spin(pre[:, :turned], cos_ref[rows, :], sin_ref[rows, :]).astype(BF16)
        for h in range(per_group):
            q_ref[h, rows, :] = spun[:, h * HEAD_DIM : (h + 1) * HEAD_DIM]
        k_ref[rows, :] = spun[:, query_width:turned]
        v_ref[rows, :] = pre[:, turned : turned + HEAD_DIM].astype(BF16)
        return carry

    lax.fori_loop(0, length // BLOCK, project, 0)
    for i in range(length // BLOCK):
        seen = (i + 1) * BLOCK
        rows = slice(i * BLOCK, seen)
        keys, values = k_ref[:seen, :], v_ref[:seen, :]
        for h in range(per_group):
            scores = dot(q_ref[h, rows, :], keys, (1, 1)) * ATTENTION_SCALE
            peak = jnp.max(scores, axis=1, keepdims=True)
            lifted = jnp.exp(scores - peak)
            total = jnp.sum(lifted, axis=1, keepdims=True)
            weights = (lifted * (1.0 / total)).astype(BF16)
            mixed = dot(weights, values)
            o_ref[rows, h * HEAD_DIM : (h + 1) * HEAD_DIM] = mixed.astype(BF16)
            lse_ref[h, rows, :] = peak + jnp.log(total)
        part_ref[rows, :] = dot(o_ref[rows, :], w_out_ref[:query_width, :]).astype(BF16)


def attend(x_all, w_in, w_out, cosine, sine, per_group):
    length, model_width = x_all.shape
    query_width = per_group * HEAD_DIM
    shapes = [
        jax.ShapeDtypeStruct((length, model_width), BF16),
        jax.ShapeDtypeStruct((length, model_width), BF16),
        jax.ShapeDtypeStruct((per_group, length, HEAD_DIM), BF16),
        jax.ShapeDtypeStruct((length, HEAD_DIM), BF16),
        jax.ShapeDtypeStruct((length, HEAD_DIM), BF16),
        jax.ShapeDtypeStruct((length, query_width), BF16),
        jax.ShapeDtypeStruct((per_group, length, 1), F32),
    ]
    return pl.pallas_call(
        functools.partial(attend_kernel, per_group),
        out_shape=shapes,
        in_specs=[pl.BlockSpec(memory_space=pltpu.VMEM)] * 5,
        out_specs=[pl.BlockSpec(memory_space=pltpu.VMEM)] * len(shapes),
        compiler_params=pltpu.CompilerParams(vmem_limit_bytes=VMEM_LIMIT),
        cost_estimate=pl.CostEstimate(
            flops=8_000_000_000, bytes_accessed=16_000_000, transcendentals=2_000_000
        ),
        name="attend",
    )(x_all, w_in, w_out, cosine, sine)


def attend_back_kernel(per_group, *refs):
    attend_back_steps(per_group, lambda step: None, *refs)


def attend_back_talk_kernel(per_group, size, swaps, *refs):
    ins, refs = refs[:13], refs[13:]
    sum_ref, sent, refs = refs[0], refs[1 : 1 + swaps], refs[1 + swaps :]
    part_ref, gin_ref, out_low, e_own, e_other = refs[:5]
    came, refs = refs[5 : 5 + swaps], refs[5 + swaps :]
    scratch, stage_a, stage_b, refs = refs[:5], refs[5:11], refs[11:17], refs[17:]
    gout_ref, line_sums, line_landed, sends, receives, swap_sems, line_send, line_recv = refs
    plane, line = plane_neighbours(), lax.axis_index("fsdp")
    other = Scatter(plane, 0, sum_ref, 8, stage_a, sends, receives)
    mine = Scatter(plane, 1, sum_ref, 0, stage_b, sends, receives)
    gout = LineScatter(line, size, 0, gout_ref, line_sums, line_landed, line_send, line_recv)
    across = [
        push(source, target, swap_sems.at[0, i], swap_sems.at[1, i], "fsdp", pair_of(line))
        for i, (source, target) in enumerate(zip(sent, came))
    ]
    half = e_own.shape[0] // 2

    def hook(step):
        if step == 0:
            meet(plane, line, size, True)
            other.begin()
            mine.begin()
            gout.begin()
            across[0].start()
        elif step == 1:
            other.first()
            gout.step(0)
            for copy in across[1:2]:
                copy.start()
        elif step == 2:
            mine.first()
            gout.step(1)
            for copy in across[2:]:
                copy.start()
        elif step == 3:
            other.second()
            gout.step(2)
        elif step == 4:
            mine.second()
        elif step == 6:
            for h in range(2):
                e_other[pl.ds(h * half, half)] = other.total(h).astype(BF16)
                e_own[pl.ds(h * half, half)] = mine.total(h)
            out_low[...] = gout.total().astype(BF16)
            for item in (other, mine, gout):
                item.finish()
            for copy in across:
                copy.wait()

    attend_back_steps(per_group, hook, *ins, part_ref, gin_ref, gout_ref, *scratch)


def attend_back_steps(
    per_group, hook, dw_ref, w_in_ref, w_out_ref, cos_ref, sin_ref,
    a_ref, q_ref, k_ref, v_ref, o_ref, lse_ref, b_all_ref, dl_ref,
    part_ref, gin_ref, gout_ref,
    turn_ref, dv_ref, back_ref, b_ref, b_sem,
):
    length, model_width = dw_ref.shape
    fetch = pltpu.make_async_copy(b_all_ref.at[pl.ds(0, length)], b_ref, b_sem)
    fetch.start()
    query_width = per_group * HEAD_DIM
    turned = query_width + HEAD_DIM
    blocks = length // BLOCK
    chunk = 384

    def out_grads(i, carry):
        columns = pl.ds(pl.multiple_of(i * chunk, chunk), chunk)
        gout_ref[i] = dot(o_ref[...], dw_ref[:, columns], (0, 0)).astype(BF16)
        return carry

    lax.fori_loop(0, model_width // chunk, out_grads, 0)
    hook(0)
    turn_ref[...] = jnp.zeros_like(turn_ref)
    dv_ref[...] = jnp.zeros_like(dv_ref)
    for i in range(blocks):
        seen = (i + 1) * BLOCK
        rows = slice(i * BLOCK, seen)
        keys, values = k_ref[:seen, :], v_ref[:seen, :]
        grad = dot(dw_ref[rows, :], w_out_ref[:query_width, :], (1, 1)).astype(BF16)
        for h in range(per_group):
            columns = slice(h * HEAD_DIM, (h + 1) * HEAD_DIM)
            queries = q_ref[h, rows, :]
            grad_head = grad[:, columns]
            scores = dot(queries, keys, (1, 1)) * ATTENTION_SCALE
            probs = jnp.exp(scores - lse_ref[h, rows, :])
            dv_ref[:seen, :] += dot(probs.astype(BF16), grad_head, (0, 0))
            grad_probs = dot(grad_head, values, (1, 1))
            inner = jnp.sum(probs * grad_probs, axis=1, keepdims=True)
            grad_scores = (probs * (grad_probs - inner)).astype(BF16)
            turn_ref[rows, columns] = dot(grad_scores, keys) * ATTENTION_SCALE
            turn_ref[:seen, query_width:turned] += (
                dot(grad_scores, queries, (0, 0)) * ATTENTION_SCALE
            )
        hook(1 + i)

    def unturn(i, carry):
        rows = pl.ds(pl.multiple_of(i * BLOCK, BLOCK), BLOCK)
        back_ref[rows, :turned] = spin(
            turn_ref[rows, :], cos_ref[rows, :], -sin_ref[rows, :]
        ).astype(BF16)
        back_ref[rows, turned:] = jnp.concatenate(
            [dv_ref[rows, :].astype(BF16), jnp.zeros((BLOCK, LANES - HEAD_DIM), BF16)], axis=1
        )
        part_ref[rows, :] = dot(
            back_ref[rows, : turned + HEAD_DIM], w_in_ref[:, : turned + HEAD_DIM], (1, 1)
        ).astype(BF16)
        return carry

    lax.fori_loop(0, blocks, unturn, 0)
    hook(5)
    fetch.wait()

    def weight_grads(i, carry):
        columns = pl.ds(pl.multiple_of(i * chunk, chunk), chunk)
        a = a_ref[:, columns]
        gin_ref[columns, :turned] = dot(a, back_ref[:, :turned], (0, 0)).astype(BF16)
        gin_ref[columns, turned:] = (
            dot(a, back_ref[:, turned:], (0, 0)) + dot(b_ref[:, columns], dl_ref[...], (0, 0))
        ).astype(BF16)
        return carry

    lax.fori_loop(0, model_width // chunk, weight_grads, 0)
    hook(6)


def attend_back(
    dw_all, w_in, w_out, cosine, sine, saved, b_all, dl_all, per_group, talk=None, collective_id=None
):
    length, model_width = dw_all.shape
    query_width = per_group * HEAD_DIM
    turned = query_width + HEAD_DIM
    shapes = [
        jax.ShapeDtypeStruct((length, model_width), BF16),
        jax.ShapeDtypeStruct((model_width, w_in.shape[1]), BF16),
        jax.ShapeDtypeStruct((model_width // 384, query_width, 384), BF16),
    ]
    scratch = [
        pltpu.VMEM((length, turned), F32),
        pltpu.VMEM((length, HEAD_DIM), F32),
        pltpu.VMEM((length, w_in.shape[1]), BF16),
        pltpu.VMEM((length, model_width), BF16),
        pltpu.SemaphoreType.DMA,
    ]
    operands = (dw_all, w_in, w_out, cosine, sine, *saved, b_all, dl_all)
    in_specs, out_specs = in_vmem(11) + anywhere(1) + in_vmem(1), in_vmem(len(shapes))
    kernel = functools.partial(attend_back_kernel, per_group)
    params = pltpu.CompilerParams(vmem_limit_bytes=VMEM_LIMIT)
    if talk is not None:
        sum_part, sent = talk
        wide = sum_part.shape[1:]
        shapes = shapes + [jax.ShapeDtypeStruct(wide, F32), jax.ShapeDtypeStruct(wide, BF16)]
        shapes += [jax.ShapeDtypeStruct(array.shape, array.dtype) for array in sent]
        gout_shape, size = shapes[2].shape, lax.axis_size("fsdp")
        shapes[2] = jax.ShapeDtypeStruct(gout_shape[1:], BF16)
        scratch = scratch + scatter_scratch(*wide, BF16) * 2
        scratch += [pltpu.VMEM(gout_shape, BF16)] + [pltpu.VMEM((2,) + gout_shape, BF16)] * 2
        scratch += scatter_sems(2) + [pltpu.SemaphoreType.DMA((2, len(sent)))]
        scratch += line_scatter_sems(1, size)
        operands += (sum_part, *sent)
        in_specs = in_specs + in_vmem(1) + anywhere(len(sent))
        out_specs = out_specs + in_vmem(2) + anywhere(len(sent))
        kernel = functools.partial(attend_back_talk_kernel, per_group, size, len(sent))
        params = talk_params(collective_id)
    return pl.pallas_call(
        kernel,
        out_shape=shapes,
        in_specs=in_specs,
        out_specs=out_specs,
        scratch_shapes=scratch,
        compiler_params=params,
        cost_estimate=pl.CostEstimate(
            flops=20_000_000_000, bytes_accessed=30_000_000, transcendentals=2_000_000
        ),
        name="attend_back",
    )(*operands)


def experts_kernel(
    here, tile,
    place_ref, b_hbm, dy_hbm, g_ref, gate_hbm, up_hbm, down_hbm, *rest,
):
    out_hbm, db_hbm, dg_ref = rest[:3]
    grad_hbm, rest = rest[3:6], rest[6:]
    (
        b_ref, dy_ref, in_ref, down_ref, hidden_ref, back_ref, out_ref, db_ref,
        gate_stage, up_stage, down_stage, weight_sem, tile_sem, out_sem, grad_sem,
    ) = rest
    rows_all, model_width = b_ref.shape
    width = down_ref.shape[0] // here
    tiles = rows_all // tile
    first = place_ref[0]

    def columns_of(e):
        return slice(e * width, (e + 1) * width)

    loads = []
    for e in range(here):
        loads.append((gate_hbm.at[e], in_ref.at[:, columns_of(e)]))
        loads.append((up_hbm.at[e], in_ref.at[:, columns_of(here + e)]))
    for e in range(here):
        loads.append((down_hbm.at[e], down_ref.at[columns_of(e), :]))
    loads = [
        pltpu.make_async_copy(source, target, weight_sem.at[i])
        for i, (source, target) in enumerate(loads)
    ]

    def tile_rows(i):
        return pl.ds(pl.multiple_of(i * tile, tile), tile)

    def tile_load(i, k):
        source, target = ((b_hbm, b_ref), (dy_hbm, dy_ref))[k]
        return pltpu.make_async_copy(
            source.at[tile_rows(i)], target.at[tile_rows(i)], tile_sem.at[k, i]
        )

    def tile_store(i, k):
        source, target = ((out_ref, out_hbm), (db_ref, db_hbm))[k]
        return pltpu.make_async_copy(
            source.at[tile_rows(i)], target.at[tile_rows(i)], out_sem.at[k, i]
        )

    for k in range(2):
        tile_load(0, k).start()
    for load in loads:
        load.start()
    for i in range(1, tiles):
        for k in range(2):
            tile_load(i, k).start()
    for load in loads:
        load.wait()

    def forward_back(i, carry):
        rows = tile_rows(i)
        tile_load(i, 0).wait()
        tile_load(i, 1).wait()
        pre = dot(b_ref[rows, :], in_ref[...])
        grad_mixed = dot(dy_ref[rows, :], down_ref[...], (1, 1))
        gates = g_ref[rows, :]
        lane = lax.broadcasted_iota(jnp.int32, gates.shape, 1)
        inner = jnp.zeros(gates.shape, F32)
        for e in range(here):
            mine = lane == first + e
            gate = jnp.sum(jnp.where(mine, jnp.maximum(gates, 0.0), 0.0), axis=1, keepdims=True)
            scale = RESIDUAL_SCALE * gate
            gate_pre, up_pre = pre[:, columns_of(e)], pre[:, columns_of(here + e)]
            sigmoid = 1.0 / (1.0 + jnp.exp(-gate_pre))
            silu = gate_pre * sigmoid
            hidden = silu * up_pre
            grad = grad_mixed[:, columns_of(e)]
            share = jnp.sum(hidden * grad, axis=1, keepdims=True)
            inner = jnp.where(mine, RESIDUAL_SCALE * share, inner)
            hidden_ref[rows, columns_of(e)] = (scale * hidden).astype(BF16)
            grad = scale * grad
            back_ref[rows, columns_of(e)] = (
                grad * up_pre * sigmoid * (1.0 + gate_pre * (1.0 - sigmoid))
            ).astype(BF16)
            back_ref[rows, columns_of(here + e)] = (grad * silu).astype(BF16)
        dg_ref[rows, :] = inner
        db_ref[rows, :] = dot(back_ref[rows, :], in_ref[...], (1, 1)).astype(BF16)
        tile_store(i, 1).start()
        out_ref[rows, :] = dot(hidden_ref[rows, :], down_ref[...]).astype(BF16)
        tile_store(i, 0).start()
        return carry

    lax.fori_loop(0, tiles, forward_back, 0)
    parts = 4
    part = model_width // parts

    def part_columns(i):
        return pl.ds(pl.multiple_of(i * part, part), part)

    def down_grad(i, carry):
        grad = dot(hidden_ref[...], dy_ref[:, part_columns(i)], (0, 0))
        for e in range(here):
            down_stage[i, e] = grad[columns_of(e), :].astype(BF16)
        return carry

    def in_grad(i, carry):
        grad = dot(b_ref[:, part_columns(i)], back_ref[...], (0, 0))
        for e in range(here):
            gate_stage[i, e] = grad[:, columns_of(e)].astype(BF16)
            up_stage[i, e] = grad[:, columns_of(here + e)].astype(BF16)
        return carry

    stores = []

    def store(k, stage):
        copy = pltpu.make_async_copy(stage, grad_hbm[k], grad_sem.at[k])
        copy.start()
        stores.append(copy)

    lax.fori_loop(0, parts, down_grad, 0)
    store(2, down_stage)
    lax.fori_loop(0, parts, in_grad, 0)
    store(0, gate_stage)
    store(1, up_stage)
    for copy in stores:
        copy.wait()
    for i in range(tiles):
        for k in range(2):
            tile_store(i, k).wait()


def experts(place, b_all, dy_all, g_all, w_gate, w_up, w_down):
    sources, tokens, model_width = b_all.shape
    here, _, hidden_width = w_gate.shape
    rows_all = sources * tokens
    width = hidden_width
    part = model_width // 4
    tile = 256
    tiles = rows_all // tile
    in_stage, down_stage = (4, here, part, width), (4, here, width, part)
    shapes = [in_stage, in_stage, down_stage]
    flat = (rows_all, model_width)
    out = pl.pallas_call(
        functools.partial(experts_kernel, here, tile),
        out_shape=[
            jax.ShapeDtypeStruct(flat, BF16),
            jax.ShapeDtypeStruct(flat, BF16),
            jax.ShapeDtypeStruct((rows_all, LANES), F32),
        ]
        + [jax.ShapeDtypeStruct(shape, BF16) for shape in shapes],
        in_specs=[pl.BlockSpec(memory_space=pltpu.SMEM)] + anywhere(2) + in_vmem(1) + anywhere(3),
        out_specs=anywhere(2) + in_vmem(1) + anywhere(len(shapes)),
        scratch_shapes=[
            pltpu.VMEM(flat, BF16),
            pltpu.VMEM(flat, BF16),
            pltpu.VMEM((model_width, 2 * here * width), BF16),
            pltpu.VMEM((here * width, model_width), BF16),
            pltpu.VMEM((rows_all, here * width), BF16),
            pltpu.VMEM((rows_all, 2 * here * width), BF16),
            pltpu.VMEM(flat, BF16),
            pltpu.VMEM(flat, BF16),
            pltpu.VMEM(in_stage, BF16),
            pltpu.VMEM(in_stage, BF16),
            pltpu.VMEM(down_stage, BF16),
            pltpu.SemaphoreType.DMA((3 * here,)),
            pltpu.SemaphoreType.DMA((2, tiles)),
            pltpu.SemaphoreType.DMA((2, tiles)),
            pltpu.SemaphoreType.DMA((3,)),
        ],
        compiler_params=pltpu.CompilerParams(vmem_limit_bytes=VMEM_LIMIT),
        cost_estimate=pl.CostEstimate(
            flops=43_000_000_000, bytes_accessed=42_000_000, transcendentals=1_000_000
        ),
        name="experts",
    )(
        place, b_all.reshape(flat), dy_all.reshape(flat), g_all.reshape(rows_all, LANES),
        w_gate, w_up, w_down,
    )
    return [
        out[0].reshape(b_all.shape), out[1].reshape(b_all.shape),
        out[2].reshape(sources, tokens, LANES), *out[3:],
    ]


class Trade:
    def __init__(self, line, stages, nears, came, far, sems):
        self.beside, self.across = beside(line), pair_of(line)
        self.stages, self.nears, self.came, self.far, self.sems = stages, nears, came, far, sems

    def copies(self, e, hop):
        made = []
        for k in range(3):
            source = self.stages[k].at[e, (1, 0, 3)[hop]]
            target = self.far[k] if hop == 2 else (self.nears, self.came)[hop][k].at[e]
            peer = self.across if hop == 2 else self.beside
            made.append(
                push(source, target, self.sems.at[0, hop, k, e], self.sems.at[1, hop, k, e], "fsdp", peer)
            )
        return made

    def send(self, e, hop):
        for copy in self.copies(e, hop):
            copy.start()

    def add(self, e):
        for k, copy in enumerate(self.copies(e, 0)):
            copy.wait_recv()
            self.stages[k][e, 3] = (
                self.stages[k][e, 3].astype(F32) + self.nears[k][e].astype(F32)
            ).astype(BF16)

    def finish(self, count):
        for e in range(count):
            for hop in range(3 if e == 0 else 2):
                for copy in self.copies(e, hop):
                    copy.wait_send()
                    if hop:
                        copy.wait_recv()


def experts_back_kernel(
    here, tile, lane_of, query_width, router_at,
    b_hbm, dy_hbm, g_ref, gate_hbm, up_hbm, down_hbm,
    middle_ref, marked_ref, win_ref, wout_ref,
    out_hbm, dw_out, dl_out, grad_ref, gain_ref, *rest,
):
    kept_hbm, came_hbm, far_hbm, rest = rest[0:3], rest[3:6], rest[6:9], rest[9:]
    other_hbm, rest = rest[: 3 * (here - 1)], rest[3 * (here - 1) :]
    (
        b_ref, dy_ref, in_ref, down_ref, hidden_ref, back_ref, out_ref, db_ref, dg_ref,
        down_stage, gate_stage, up_stage, down_near, gate_near, up_near,
        dw_own, dl_own, db_total, dg_total, db_landed, dg_landed,
    ) = rest[:21]
    scratch, rest = rest[21:41], rest[41:]
    (
        weight_sem, tile_sem, out_sem, kept_sem, other_sem, trade_sems, swap_sems,
        scatter_send, scatter_recv, own_sem, send_sem, recv_sem,
    ) = rest
    rows_all, model_width = b_ref.shape
    width = down_ref.shape[1]
    tiles = rows_all // tile
    tokens = middle_ref.shape[0]
    per_tile = tile // tokens
    plane, line = plane_neighbours(), lax.axis_index("fsdp")
    me = plane[0]
    first = me * here + lane_of
    high, low = line // 2, lax.rem(line, 2)
    span = pl.ds(pl.multiple_of(high * width, width), width)

    def weight_loads(e):
        pairs = (
            (gate_hbm.at[e, :, span], in_ref.at[e, :, pl.ds(0, width)]),
            (up_hbm.at[e, :, span], in_ref.at[e, :, pl.ds(width, width)]),
            (down_hbm.at[e, span, :], down_ref.at[e]),
        )
        return [
            pltpu.make_async_copy(source, target, weight_sem.at[e, i])
            for i, (source, target) in enumerate(pairs)
        ]

    def tile_rows(j):
        return pl.ds(pl.multiple_of(j * tile, tile), tile)

    def tile_loads(j):
        return [
            pltpu.make_async_copy(
                source.at[tile_rows(j)], target.at[tile_rows(j)], tile_sem.at[k, j]
            )
            for k, (source, target) in enumerate(((b_hbm, b_ref), (dy_hbm, dy_ref)))
        ]

    def tile_store(j):
        return pltpu.make_async_copy(
            out_ref.at[tile_rows(j)], out_hbm.at[tile_rows(j)], out_sem.at[j]
        )

    def place_of(i):
        return lax.rem(i + tiles // 2, tiles)

    def start_loads(i, carry):
        for load in tile_loads(place_of(i)):
            load.start()
        return carry

    start_loads(0, 0)
    for load in weight_loads(0):
        load.start()
    lax.fori_loop(1, tiles, start_loads, 0)
    for e in range(1, here):
        for load in weight_loads(e):
            load.start()
    meet(plane, line, 4, False)
    trade = Trade(
        line, (down_stage, gate_stage, up_stage), (down_near, gate_near, up_near),
        came_hbm, far_hbm, trade_sems,
    )
    sums = (scatter_send, scatter_recv)
    db_other = Scatter(plane, 0, db_ref, 8, scratch[:5], *sums)
    dg_other = Scatter(plane, 1, dg_ref, 8, scratch[5:10], *sums)
    db = Scatter(plane, 2, db_ref, 0, scratch[10:15], *sums)
    dg = Scatter(plane, 3, dg_ref, 0, scratch[15:20], *sums)
    swap_g = push(dg_total, dg_landed, swap_sems.at[0], swap_sems.at[1], "fsdp", pair_of(line))
    swap_b = push(db_total, db_landed, swap_sems.at[2], swap_sems.at[3], "fsdp", pair_of(line))
    half = tokens // 2
    part = model_width // 4

    def one_expert(e, carry):
        for load in weight_loads(e):
            load.wait()
        last = e == here - 1

        def forward_back(i, carry):
            j = place_of(i)
            rows = tile_rows(j)

            @pl.when(e == 0)
            def _():
                for load in tile_loads(j):
                    load.wait()

            pre = dot(b_ref[rows, :], in_ref[e])
            grad = dot(dy_ref[rows, :], down_ref[e], (1, 1))
            gates = g_ref[rows, :]
            mine = lax.broadcasted_iota(jnp.int32, gates.shape, 1) == first + e
            gate = jnp.sum(jnp.where(mine, jnp.maximum(gates, 0.0), 0.0), axis=1, keepdims=True)
            scale = RESIDUAL_SCALE * gate
            gate_pre, up_pre = pre[:, :width], pre[:, width:]
            sigmoid = 1.0 / (1.0 + jnp.exp(-gate_pre))
            silu = gate_pre * sigmoid
            hidden = silu * up_pre
            share = jnp.sum(hidden * grad, axis=1, keepdims=True)
            inner = jnp.where(mine, RESIDUAL_SCALE * share, 0.0)
            hidden_ref[rows, :] = (scale * hidden).astype(BF16)
            grad = scale * grad
            back_ref[rows, :width] = (
                grad * up_pre * sigmoid * (1.0 + gate_pre * (1.0 - sigmoid))
            ).astype(BF16)
            back_ref[rows, width:] = (grad * silu).astype(BF16)
            made = dot(hidden_ref[rows, :], down_ref[e])
            back = dot(back_ref[rows, :], in_ref[e], (1, 1))

            @pl.when(e == 0)
            def _():
                out_ref[rows, :] = made.astype(BF16)
                for t in range(per_tile):
                    piece = slice(t * tokens, (t + 1) * tokens)
                    db_ref[per_tile * j + t] = back[piece].astype(BF16)
                    dg_ref[per_tile * j + t] = inner[piece]

            @pl.when(e > 0)
            def _():
                out_ref[rows, :] = (out_ref[rows, :].astype(F32) + made).astype(BF16)
                for t in range(per_tile):
                    piece = slice(t * tokens, (t + 1) * tokens)
                    block = per_tile * j + t
                    db_ref[block] = (db_ref[block].astype(F32) + back[piece]).astype(BF16)
                    dg_ref[block] += inner[piece]

            @pl.when(last)
            def _():
                tile_store(j).start()

            @pl.when((e == 1) & (i == tiles - 3))
            def _():
                trade.add(0)
                trade.send(0, 2)

            @pl.when(last & (i == tiles // 2 - 1))
            def _():
                dg_other.begin()
                db_other.begin()

            @pl.when(last & (i == tiles - 2))
            def _():
                dg_other.first()
                db_other.first()

            return carry

        lax.fori_loop(0, tiles, forward_back, 0)

        @pl.when(last)
        def _():
            dg.begin()
            db.begin()
            dg_other.second()
            db_other.second()

        def weight_grads(p, carry):
            i = p + 1 - 2 * lax.rem(p, 2)
            parity = jnp.where(p < 2, 1 - low, low)
            side = jnp.where(lax.rem(i, 2) == 0, high, 1 - high)
            columns = pl.ds(pl.multiple_of((2 * side + parity) * part, part), part)
            down_stage[e, i] = dot(hidden_ref[...], dy_ref[:, columns], (0, 0)).astype(BF16)
            grad = dot(b_ref[:, columns], back_ref[...], (0, 0))
            gate_stage[e, i] = grad[:, :width].astype(BF16)
            up_stage[e, i] = grad[:, width:].astype(BF16)

            @pl.when((p == 0) & (e < here - 1))
            def _():
                trade.send(e, 0)

            @pl.when((p == 1) & (e < here - 2))
            def _():
                trade.send(e, 1)

            @pl.when(last & (p == 1))
            def _():
                for h in range(2):
                    rows = pl.ds(h * half, half)
                    dg_total[rows] = dg_other.total(h)
                    db_total[rows] = db_other.total(h).astype(BF16)
                swap_g.start()
                swap_b.start()
                trade.send(here - 2, 1)
                trade.send(here - 1, 0)
                trade.send(here - 1, 1)

            @pl.when(last & (p == 2))
            def _():
                dg.first()
                db.first()

            return carry

        lax.fori_loop(0, 4, weight_grads, 0)
        return carry

    lax.fori_loop(0, here, one_expert, 0)
    stores = [
        pltpu.make_async_copy(stage.at[e, 2], kept_hbm[k].at[e], kept_sem.at[k, e])
        for k, stage in enumerate((down_stage, gate_stage, up_stage))
        for e in range(here)
    ]
    for store in stores:
        store.start()
    dg.second()
    db.second()
    others = []

    def give_other(e):
        trade.add(e)
        for k, stage in enumerate((down_stage, gate_stage, up_stage)):
            target = other_hbm[3 * (e - 1) + k]
            others.append(pltpu.make_async_copy(stage.at[e, 3], target, other_sem.at[e - 1, k]))
            others[-1].start()

    for e in range(1, here - 1):
        give_other(e)
    gain = wout_ref[query_width + 1 : query_width + 2, :].astype(F32)
    router = win_ref[:, router_at : router_at + LANES]
    gain_grad = jnp.zeros((1, model_width), F32)
    sums_g = [dg.total(h) for h in range(2)]
    swap_g.wait_recv()
    swap_b.wait_recv()
    for h in range(2):
        rows = pl.ds(h * half, half)
        gates = jnp.maximum(marked_ref[rows], 0.0)
        grad_gates = sums_g[h] + dg_landed[rows]
        grad_chosen = gates * (
            grad_gates - jnp.sum(gates * grad_gates, axis=1, keepdims=True)
        )
        grad_logits = grad_chosen.astype(BF16)
        dl_own[rows] = grad_logits
        grad_b = dot(grad_logits, router, (1, 1)) + db.total(h) + db_landed[rows].astype(F32)
        middle = middle_ref[rows]
        inverse = lax.rsqrt(jnp.mean(middle * middle, axis=1, keepdims=True) + EPSILON)
        normed = middle * inverse
        gain_grad += jnp.sum(grad_b * normed, axis=0, keepdims=True)
        own = pl.ds(pl.multiple_of(me * tokens + h * half, half), half)
        grad = dy_ref[own].astype(F32) + norm_back(grad_b * gain, normed, inverse)
        grad_ref[rows] = grad
        dw_own[rows] = (RESIDUAL_SCALE * grad).astype(BF16)
    gain_ref[...] = jnp.broadcast_to(gain_grad, gain_ref.shape)
    gathers = (own_sem, send_sem, recv_sem)
    dw = Gather(plane, 0, dw_own, dw_out, 0, *gathers)
    dl = Gather(plane, 1, dl_own, dl_out, 0, *gathers)
    dw.begin()
    dl.begin()
    dw.relay()
    dl.relay()
    dw.relay_diagonal()
    dl.relay_diagonal()
    give_other(here - 1)
    for item in (dg_other, db_other, dg, db, dw, dl):
        item.finish()
    swap_b.wait_send()
    swap_g.wait_send()
    for store in stores + others:
        store.wait()
    for j in range(tiles):
        tile_store(j).wait()
    trade.finish(here)


def experts_back(
    b_all, dy_all, g_all, w_gate, w_up, w_down, middle, marked, w_in, w_out,
    lane_of, query_width, router_at, collective_id,
):
    sources, tokens, model_width = b_all.shape
    here, _, hidden_width = w_gate.shape
    rows_all = sources * tokens
    width, part, tile = hidden_width // 2, model_width // 4, 256
    tiles = rows_all // tile
    flat, wide, narrow = (rows_all, model_width), (tokens, model_width), (tokens, LANES)
    slices = [(width, part), (part, width), (part, width)]
    out = pl.pallas_call(
        functools.partial(experts_back_kernel, here, tile, lane_of, query_width, router_at),
        out_shape=[
            jax.ShapeDtypeStruct(flat, BF16),
            jax.ShapeDtypeStruct((8,) + wide, BF16),
            jax.ShapeDtypeStruct((8,) + narrow, BF16),
            jax.ShapeDtypeStruct(wide, F32),
            jax.ShapeDtypeStruct((8, model_width), F32),
        ]
        + [jax.ShapeDtypeStruct((here,) + shape, BF16) for shape in slices * 2]
        + [jax.ShapeDtypeStruct(shape, BF16) for shape in slices * here],
        in_specs=anywhere(2) + in_vmem(1) + anywhere(3) + in_vmem(4),
        out_specs=anywhere(3) + in_vmem(2) + anywhere(6 + 3 * here),
        scratch_shapes=[
            pltpu.VMEM(flat, BF16),
            pltpu.VMEM(flat, BF16),
            pltpu.VMEM((here, model_width, 2 * width), BF16),
            pltpu.VMEM((here, width, model_width), BF16),
            pltpu.VMEM((rows_all, width), BF16),
            pltpu.VMEM((rows_all, 2 * width), BF16),
            pltpu.VMEM(flat, BF16),
            pltpu.VMEM((sources,) + wide, BF16),
            pltpu.VMEM((sources,) + narrow, F32),
        ]
        + [pltpu.VMEM((here, 4) + shape, BF16) for shape in slices]
        + [pltpu.VMEM((here,) + shape, BF16) for shape in slices]
        + [
            pltpu.VMEM(wide, BF16),
            pltpu.VMEM(narrow, BF16),
            pltpu.VMEM(wide, BF16),
            pltpu.VMEM(narrow, F32),
            pltpu.VMEM(wide, BF16),
            pltpu.VMEM(narrow, F32),
        ]
        + (scatter_scratch(*wide, BF16, True) + scatter_scratch(*narrow, F32, True)) * 2
        + [
            pltpu.SemaphoreType.DMA((here, 3)),
            pltpu.SemaphoreType.DMA((2, tiles)),
            pltpu.SemaphoreType.DMA((tiles,)),
            pltpu.SemaphoreType.DMA((3, here)),
            pltpu.SemaphoreType.DMA((here - 1, 3)),
            pltpu.SemaphoreType.DMA((2, 3, 3, here)),
            pltpu.SemaphoreType.DMA((4,)),
        ]
        + scatter_sems(4)
        + gather_sems(2),
        compiler_params=pltpu.CompilerParams(
            collective_id=collective_id, has_side_effects=True, vmem_limit_bytes=67_000_000
        ),
        cost_estimate=pl.CostEstimate(
            flops=43_000_000_000, bytes_accessed=42_000_000, transcendentals=1_000_000
        ),
        name="experts_back",
    )(
        b_all.reshape(flat), dy_all.reshape(flat), g_all.reshape(rows_all, LANES),
        w_gate, w_up, w_down, middle, marked, w_in, w_out,
    )
    others = [out[at : at + 3] for at in range(14, 11 + 3 * here, 3)]
    return [out[0].reshape(b_all.shape), *out[1:5], out[5:8], out[8:11], out[11:14], others]


def rotary_tables(length):
    lane = lax.broadcasted_iota(jnp.int32, (length, LANES), 1) % HEAD_DIM
    half = HEAD_DIM // 2
    exponent = (lane % half).astype(F32) * (2.0 / HEAD_DIM)
    position = lax.broadcasted_iota(jnp.int32, (length, LANES), 0).astype(F32)
    angles = position * jnp.power(ROPE_BASE, -exponent)
    return jnp.cos(angles), jnp.where(lane < half, -jnp.sin(angles), jnp.sin(angles))


def finish_kernel(per_group, here, in_ref, out_ref, *refs):
    kept, came, far, refs = refs[:3], refs[3:6], refs[6 : 6 + 3 * here], refs[6 + 3 * here :]
    query_ref, key_ref, value_ref, router_ref, proj_ref, *expert_refs = refs
    query_width = per_group * HEAD_DIM
    groups, out_rows, _ = out_ref.shape
    for j in range(0, groups, 2):
        pair = (in_ref[j].astype(F32), in_ref[j + 1].astype(F32))
        at = 0
        for target, width in ((query_ref, query_width), (key_ref, HEAD_DIM), (value_ref, HEAD_DIM)):
            target[:, j * width : (j + 2) * width] = jnp.concatenate(
                [block[:, at : at + width] for block in pair], axis=1
            )
            at += width
    router_ref[...] = in_ref[0][:, at : at + router_ref.shape[1]].astype(F32)
    for j in range(groups):
        proj_ref[j * out_rows : (j + 1) * out_rows, :] = out_ref[j].astype(F32)
    high = lax.axis_index("fsdp") // 2
    for k, target in enumerate(expert_refs):
        width = kept[k].shape[1 if k == 0 else 2]
        near = pl.ds(pl.multiple_of(high * width, width), width)
        beyond = pl.ds(pl.multiple_of((1 - high) * width, width), width)
        for e in range(here):
            near_sum = kept[k][e].astype(F32) + came[k][e].astype(F32)
            far_sum = far[3 * e + k][...].astype(F32)
            if k == 0:
                target[e, near, :] = near_sum
                target[e, beyond, :] = far_sum
            else:
                target[e, :, near] = near_sum
                target[e, :, beyond] = far_sum


def finish(in_all, out_all, kept, came, far, per_group, experts_all):
    groups, shard, _ = in_all.shape
    here, width, part = kept[0].shape
    query_width = per_group * HEAD_DIM
    shapes = [
        (shard, groups * query_width),
        (shard, groups * HEAD_DIM),
        (shard, groups * HEAD_DIM),
        (shard, experts_all),
        (groups * out_all.shape[1], out_all.shape[2]),
        (here, 2 * width, part),
        (here, part, 2 * width),
        (here, part, 2 * width),
    ]
    operands = (in_all, out_all, *kept, *came, *far)
    return pl.pallas_call(
        functools.partial(finish_kernel, per_group, here),
        out_shape=[jax.ShapeDtypeStruct(shape, F32) for shape in shapes],
        in_specs=in_vmem(len(operands)),
        out_specs=in_vmem(len(shapes)),
        compiler_params=pltpu.CompilerParams(vmem_limit_bytes=VMEM_LIMIT),
        cost_estimate=pl.CostEstimate(flops=0, bytes_accessed=25_000_000, transcendentals=0),
        name="finish",
    )(*operands)


def per_device(
    residual_in, cotangent, gain_attn, w_query, w_key, w_value, w_out, gain_ffn, w_router,
    w_gate, w_up, w_down, route_ids,
):
    me = lax.axis_index("expert")
    line = lax.axis_index("fsdp")
    peers = lax.axis_size("expert")
    lines = lax.axis_size("fsdp")
    tokens, model_width = residual_in.shape[1:]
    length = tokens * peers
    groups = w_key.shape[1] // HEAD_DIM
    per_group = w_query.shape[1] // w_key.shape[1]
    query_width = per_group * HEAD_DIM
    experts_all = w_router.shape[1]
    here = w_gate.shape[0]
    shard = w_query.shape[0]
    turned = query_width + HEAD_DIM
    router_at = turned
    lane_of = HEAD_DIM
    in_width = turned + LANES
    paired = lines == 4 and peers == 8

    w_in_shard = jnp.concatenate(
        [
            lax.dynamic_slice(w_query, (0, me * query_width), (shard, query_width)),
            lax.dynamic_slice(w_key, (0, me * HEAD_DIM), (shard, HEAD_DIM)),
            lax.dynamic_slice(w_value, (0, me * HEAD_DIM), (shard, HEAD_DIM)),
            w_router,
            jnp.zeros((shard, in_width - turned - HEAD_DIM - experts_all), BF16),
        ],
        axis=1,
    )
    w_out_shard = jnp.concatenate(
        [
            lax.dynamic_slice(w_out, (me * query_width, 0), (query_width, shard)),
            gain_attn[None],
            gain_ffn[None],
            jnp.zeros((14, shard), BF16),
        ],
        axis=0,
    )
    chosen = jnp.any(
        route_ids[0][:, :, None]
        == jnp.arange(LANES, dtype=jnp.int32)[None, None, :] - lane_of,
        axis=1,
    ).astype(F32)
    cosine, sine = rotary_tables(length)
    place = jnp.full((1,), me * here + lane_of, jnp.int32)
    own_rows, own_grad = residual_in[0], cotangent[0]
    wide = (peers, tokens, model_width)

    if paired:
        x_all, dy_all, w_in, w_out_rows = open_transfers(
            own_rows, own_grad, w_in_shard, w_out_shard, lines, 0
        )
    else:
        x_all, dy_all = plane_gather([own_rows, own_grad], 0)
        w_in, w_out_rows = (
            lax.all_gather(w_in_shard, "fsdp", axis=0, tiled=True),
            lax.all_gather(w_out_shard, "fsdp", axis=1, tiled=True),
        )
    part, *saved = attend(
        x_all.reshape(length, model_width), w_in, w_out_rows, cosine, sine, per_group
    )
    if paired:
        b_all, g_all, middle, marked = middle_transfers(
            part.reshape(wide), own_rows, w_in, w_out_rows, chosen, query_width, router_at, 1
        )
        sum_part, dw_all, dl_all, grad_middle, gain_two_grad, kept, came, far, others = experts_back(
            b_all, dy_all, g_all, w_gate, w_up, w_down, middle, marked, w_in, w_out_rows,
            lane_of, query_width, router_at, 2,
        )
        early = [array for given in others[:-1] for array in given]
        da_part, grad_in, out_low, e_own, e_total, *crossed = attend_back(
            dw_all.reshape(length, model_width), w_in, w_out_rows, cosine, sine, saved,
            b_all.reshape(2 * length, model_width), dl_all.reshape(length, LANES), per_group,
            (sum_part, early), 4,
        )
        outcome, grad_input, in_all, out_all, gains_all, notes_all, *crossed_last = close_transfers(
            da_part.reshape(wide), e_own, e_total, own_rows, middle, grad_middle, gain_two_grad,
            w_out_rows, grad_in.reshape(lines, shard, in_width), out_low, others[-1],
            query_width, 3,
        )
        squares = jnp.sum(notes_all, axis=0)[:5, 0]
        query, key, value, router_grad, proj, down, gate, up = finish(
            in_all, out_all, kept, came, [*far, *crossed, *crossed_last], per_group, experts_all
        )
        reduced = [gate, up, down]
        gain_rows = jnp.sum(gains_all[:, :2].astype(F32), axis=0)
    else:
        (branch,) = plane_scatter([part.reshape(wide)], 1)
        gain_one = w_out_rows[query_width][None].astype(F32)
        gain_two = w_out_rows[query_width + 1][None].astype(F32)
        router = w_in[:, router_at:]
        rows = own_rows.astype(F32)
        inverse_one = lax.rsqrt(jnp.mean(rows * rows, axis=-1, keepdims=True) + EPSILON)
        normed_one = rows * inverse_one
        middle = rows + RESIDUAL_SCALE * branch
        inverse_two = lax.rsqrt(jnp.mean(middle * middle, axis=-1, keepdims=True) + EPSILON)
        normed_two = middle * inverse_two
        routed = (normed_two * gain_two).astype(BF16)
        logits = jnp.where(chosen > 0, dot(routed, router), -1e30)
        lifted = jnp.exp(logits - jnp.max(logits, axis=-1, keepdims=True))
        lifted = jnp.where(chosen > 0, lifted, 0.0)
        gates = lifted / jnp.sum(lifted, axis=-1, keepdims=True)
        b_all, g_all = plane_gather([routed, jnp.where(chosen > 0, gates, -1.0)], 2)
        sum_part, db_part, dg_part, *grads = experts(
            place, b_all, dy_all, g_all, w_gate, w_up, w_down
        )
        db_sum, dg_sum = plane_scatter([db_part, dg_part], 3)
        grad_rows = own_grad.astype(F32)
        grad_chosen = gates * (dg_sum - jnp.sum(gates * dg_sum, axis=-1, keepdims=True))
        grad_logits = grad_chosen.astype(BF16)
        grad_routed = dot(grad_logits, router, (1, 1)) + db_sum
        grad_gain_two = jnp.sum(grad_routed * normed_two, axis=0)
        grad_middle = grad_rows + norm_back(grad_routed * gain_two, normed_two, inverse_two)
        grad_branch = (RESIDUAL_SCALE * grad_middle).astype(BF16)
        dw_all, dl_all = plane_gather([grad_branch, grad_logits], 4)
        da_part, grad_in, grad_out = attend_back(
            dw_all.reshape(length, model_width), w_in, w_out_rows, cosine, sine, saved,
            b_all.reshape(length, model_width), dl_all.reshape(length, LANES), per_group,
        )
        da_sum, expert_sum = plane_scatter([da_part.reshape(wide), sum_part], 5)
        outcome = middle + expert_sum
        grad_gain_one = jnp.sum(da_sum * normed_one, axis=0)
        grad_input = grad_middle + norm_back(da_sum * gain_one, normed_one, inverse_one)
        squares = lax.psum(
            jnp.stack(
                [jnp.sum(v * v) for v in (rows, middle, outcome, grad_middle, grad_input)]
            ),
            ("fsdp", "expert"),
        )
        in_sum = lax.psum_scatter(grad_in, "fsdp", scatter_dimension=0, tiled=True)
        out_sum = lax.psum_scatter(
            grad_out.transpose(1, 0, 2).reshape(query_width, model_width), "fsdp",
            scatter_dimension=1, tiled=True,
        )
        gain_rows = lax.psum_scatter(
            lax.psum(jnp.stack([grad_gain_one, grad_gain_two]), "expert"),
            "fsdp", scatter_dimension=1, tiled=True,
        )
        in_all = lax.all_gather(in_sum, "expert", axis=0)
        out_all = lax.all_gather(out_sum, "expert", axis=0)
        outcome, grad_input = outcome.astype(BF16), grad_input.astype(BF16)
        grads = [
            grads[0].transpose(1, 0, 2, 3).reshape(w_gate.shape),
            grads[1].transpose(1, 0, 2, 3).reshape(w_up.shape),
            grads[2].transpose(1, 2, 0, 3).reshape(w_down.shape),
        ]
        reduced = [
            lax.psum_scatter(array, "fsdp", scatter_dimension=axis, tiled=True).astype(F32)
            for array, axis in zip(grads, (1, 1, 2))
        ]

        def columns_of(start, stop):
            return in_all[:, :, start:stop].transpose(1, 0, 2).reshape(shard, -1).astype(F32)

        query, key = columns_of(0, query_width), columns_of(query_width, turned)
        value = columns_of(turned, turned + HEAD_DIM)
        proj = out_all.reshape(groups * query_width, shard).astype(F32)
        at = turned + HEAD_DIM
        router_grad = in_all[0, :, at : at + experts_all].astype(F32)

    root_means = jnp.sqrt(squares / (tokens * model_width * lines * peers))
    return (
        outcome[None],
        grad_input[None],
        gain_rows[0],
        query,
        key,
        value,
        proj,
        gain_rows[1],
        router_grad,
        reduced[0],
        reduced[1],
        reduced[2],
        root_means,
    )


def solution(mesh):
    in_specs = (
        P("fsdp", "expert", None),
        P("fsdp", "expert", None),
        P("fsdp"),
        P("fsdp", None),
        P("fsdp", None),
        P("fsdp", None),
        P(None, "fsdp"),
        P("fsdp"),
        P("fsdp", None),
        P("expert", None, None),
        P("expert", None, None),
        P("expert", None, None),
        P("fsdp", "expert", None),
    )
    out_specs = (
        P("fsdp", "expert", None),
        P("fsdp", "expert", None),
        P("fsdp"),
        P("fsdp", None),
        P("fsdp", None),
        P("fsdp", None),
        P(None, "fsdp"),
        P("fsdp"),
        P("fsdp", None),
        P("expert", "fsdp", None),
        P("expert", "fsdp", None),
        P("expert", None, "fsdp"),
        P(),
    )
    return jax.shard_map(
        per_device, mesh=mesh, in_specs=in_specs, out_specs=out_specs, check_vma=False
    )
```

profile of v0, /device:TPU:0, one launch (start us, length us, event | category | flops | bytes accessed | tf_op | source)
XLA Modules:
  0.0 441.6 jit_solution(10611311438872031935)
XLA Ops:
  0.7 0.1 pad.3.clone
  0.7 0.7 broadcast_in_dim.20
  1.4 0.7 broadcast_in_dim.21
  2.1 0.8 copy.36
  2.9 0.3 compare_reduce_fusion
  3.2 0.6 convert_element_type.27.chosen_ref
  3.8 0.8 copy.35
  4.6 0.9 constant_dynamic-slice_fusion
  5.6 0.8 maximum_maximum_fusion.wout_ref
  6.3 1.1 constant_dynamic-slice_fusion.3
  7.4 1.1 constant_dynamic-slice_fusion.1
  8.5 0.9 concatenate.6.win_ref
  9.5 3.1 negate_select_fusion
  12.5 59.0 %open_transfers.1 = (bf16[8,128,1536]{2,1,0:T(8,128)(2,1)}, bf16[16,128,1536]{2,1,0:T(8,128)(2,1)}, bf16[1536,384]{1,0:T(8,128)(2,1)}, bf16[208,1536]{1,0:T(8,128)(2,1)}) custom-call(bf16[128,1536]{1,0:T(8,128)(2,1)} %bitcast.15, bf16[128,1536]{1,0:T(8,128)(2,1)} %bitcast.23, bf16[384,384]{1,0:T(8,128)(2,1)} %concatenate.6.win_ref, ...), custom_call_target="tpu_custom_call" | custom-call | bytes 120000000 | tf_op jit(solution)/shard_map/open_transfers/pallas_call | solution.py:671
  71.5 15.8 %attend.1 = (bf16[1024,1536]{1,0:T(8,128)(2,1)}, bf16[1024,1536]{1,0:T(8,128)(2,1)}, bf16[3,1024,64]{2,1,0:T(8,128)(2,1)}, bf16[1024,64]{1,0:T(8,128)(2,1)}, bf1...) custom-call(bf16[1024,1536]{1,0:T(8,128)(2,1)} %bitcast.28, ...), custom_call_target="tpu_custom_call" | custom-call | flops 8000000000 | bytes 16000000 | tf_op jit(solution)/shard_map/attend/pallas_call | solution.py:1026
  87.3 66.0 %middle_transfers.1 = (bf16[16,128,1536]{2,1,0:T(8,128)(2,1)}, f32[16,128,128]{2,1,0:T(8,128)}, f32[128,1536]{1,0:T(8,128)}, f32[128,128]{1,0:T(8,128)}) custom-call(bf16[8,128,1536]{2,1,0:T(8,128)(2,1)} %bitcast.19, bf16[128,1536]{1,0:T(8,128)(2,1)} %bitcast.16, bf16[1536,384]{1,0:T(8,128)(2,1)} %get-tuple-element.74.w_in_ref.win_ref.refs_1_, ...), custom_call_target="tpu_custom_call" | custom-call | bytes 150000000 | tf_op jit(solution)/shard_map/middle_transfers/pallas_call | solution.py:749
  153.4 125.4 %experts_back.1 = (bf16[2048,1536]{1,0:T(8,128)(2,1)}, bf16[8,128,1536]{2,1,0:T(8,128)(2,1)}, bf16[8,128,128]{2,1,0:T(8,128)(2,1)}, f32[128,1536]{1,0:T(8,128)},...) custom-call(bf16[2048,1536]{1,0:T(8,128)(2,1)} %bitcast.25, ...), custom_call_target="tpu_custom_call" | custom-call | flops 43000000512 | bytes 42000000 | tf_op jit(solution)/shard_map/experts_back/pallas_call | solution.py:1722
  278.8 51.4 %attend_back.1 = (bf16[1024,1536]{1,0:T(8,128)(2,1)}, bf16[1536,384]{1,0:T(8,128)(2,1)}, bf16[192,384]{1,0:T(8,128)(2,1)}, f32[128,1536]{1,0:T(8,128)}, bf16[128...) custom-call(bf16[1024,1536]{1,0:T(8,128)(2,1)} %bitcast.31, ...), custom_call_target="tpu_custom_call" | custom-call | flops 20000000000 | bytes 30000000 | tf_op jit(solution)/shard_map/attend_back/pallas_call | solution.py:1207
  330.2 96.3 %close_transfers.1 = (bf16[128,1536]{1,0:T(8,128)(2,1)}, bf16[128,1536]{1,0:T(8,128)(2,1)}, bf16[8,384,384]{2,1,0:T(8,128)(2,1)}, bf16[8,192,384]{2,1,0:T(8,128)...) custom-call(bf16[8,128,1536]{2,1,0:T(8,128)(2,1)} %bitcast.18, ...), custom_call_target="tpu_custom_call" | custom-call | bytes 200000000 | tf_op jit(solution)/shard_map/close_transfers/pallas_call | solution.py:920
  426.5 0.8 convert_reduce_fusion
  427.3 0.6 slice_reduce_fusion
  427.9 0.9 reduce_sum.19
  428.7 0.6 fusion.8
  429.4 0.0 copy-start.1
  429.4 0.0 copy-start
  429.4 9.0 %finish.1 = (f32[384,1536]{1,0:T(8,128)}, f32[384,512]{1,0:T(8,128)}, f32[384,512]{1,0:T(8,128)}, f32[384,24]{1,0:T(8,128)}, f32[1536,384]{1,0:T(8,128)}, /*inde...) custom-call(bf16[8,384,384]{2,1,0:T(8,128)(2,1)} %get-tuple-element.107.in_ref, ...), custom_call_target="tpu_custom_call" | custom-call | bytes 25000000 | tf_op jit(solution)/shard_map/finish/pallas_call | solution.py:1839
  438.4 1.6 copy.37
  440.1 0.0 copy-done.1
  440.1 0.7 copy.40
  440.8 0.0 copy-done
  440.8 0.7 copy.41
  (6 shorter events, 0.0 us)
Async XLA Ops:
  429.4 10.7 %copy-start.1 = (bf16[128,1536]{1,0:T(8,128)(2,1)S(1)}, bf16[128,1536]{1,0:T(8,128)(2,1)}, u32[]{:S(2)}) copy-start(bf16[128,1536]{1,0:T(8,128)(2,1)} %get-tuple-element.104) | copy-start | bytes 1179652
  429.4 11.4 %copy-start = (bf16[128,1536]{1,0:T(8,128)(2,1)S(1)}, bf16[128,1536]{1,0:T(8,128)(2,1)}, u32[]{:S(2)}) copy-start(bf16[128,1536]{1,0:T(8,128)(2,1)} %get-tuple-element.105) | copy-start | bytes 1179652
where the time goes:
time: 442 us
  Pallas kernels  423 us (96%)
  local copies, waits for them, and re-layouts  10.8 us (2%)
  other arithmetic  7.05 us (2%)
    pallas_call x1, Pallas kernels, experts_back(): pl.pallas_call(functools.partial(experts_back_kernel, here, tile, lane_of...  125 us
    pallas_call x1, Pallas kernels, close_transfers(): pl.pallas_call(functools.partial(close_kernel, size, query_width, len(sen...  96.3 us
    pallas_call x1, Pallas kernels, middle_transfers(): pl.pallas_call(functools.partial(middle_kernel, query_width, router_at),...  66 us
    pallas_call x1, Pallas kernels, open_transfers(): pl.pallas_call(functools.partial(open_kernel, size), out_shape=[jax.Shape...  59 us
    pallas_call x1, Pallas kernels, attend_back(): pl.pallas_call(kernel, out_shape=shapes, in_specs=in_specs, out_specs=out...  51.4 us
    pallas_call x1, Pallas kernels, attend(): pl.pallas_call(functools.partial(attend_kernel, per_group), out_shape=sha...  15.8 us
    pallas_call x1, Pallas kernels, finish(): pl.pallas_call(functools.partial(finish_kernel, per_group, here), out_sha...  9.04 us

commit v1 on v0

--- a/solution.py
+++ b/solution.py
@@ -772,21 +772,7 @@
 
 
 def close_kernel(
-    size, query_width, swaps, da_ref, e_own, e_total, x_ref, middle_ref, grad_ref, gain_two_ref, wout_ref,
-    gin_ref, out_low, *rest,
-):
-    sent, rest = rest[:swaps], rest[swaps:]
-    outcome_ref, input_grad_ref, in_out, out_out, gains_out, notes_out, *rest = rest
-    came, rest = rest[:swaps], rest[swaps:]
-    close_steps(
-        size, query_width, sent, came, da_ref, e_own, e_total, x_ref, middle_ref, grad_ref,
-        gain_two_ref, wout_ref, gin_ref, out_low,
-        outcome_ref, input_grad_ref, in_out, out_out, gains_out, notes_out, *rest,
-    )
-
-
-def close_steps(
-    size, query_width, sent, came, da_ref, e_own, e_total, x_ref, middle_ref, grad_ref,
+    size, query_width, da_ref, e_own, e_total, x_ref, middle_ref, grad_ref,
     gain_two_ref, wout_ref, gin_ref, out_low,
     outcome_ref, input_grad_ref, in_out, out_out, gains_out, notes_out,
     e_landed, gains, notes, notes_line, in_low, gain_low, notes_low, *rest,
@@ -794,17 +780,13 @@
     scratch, rest = rest[:6], rest[6:]
     line_scratch, rest = rest[:4], rest[4:]
     (
-        across_sems, swap_sems, scatter_send, scatter_recv, sum_send, sum_recv,
+        swap_sems, scatter_send, scatter_recv, sum_send, sum_recv,
         line_own, line_send, line_recv, own_sem, send_sem, recv_sem,
     ) = rest
     plane, line = plane_neighbours(), lax.axis_index("fsdp")
     meet(plane, line, size, True)
     sums = (scatter_send, scatter_recv)
     da = Scatter(plane, 0, da_ref, 0, scratch[:6], *sums)
-    across = [
-        push(source, target, across_sems.at[0, i], across_sems.at[1, i], "fsdp", pair_of(line))
-        for i, (source, target) in enumerate(zip(sent, came))
-    ]
     swap = push(e_total, e_landed, swap_sems.at[0], swap_sems.at[1], "fsdp", pair_of(line))
     gin = LineScatter(line, size, 0, gin_ref, *line_scratch[0:2], sum_send, sum_recv)
     gain = LineScatter(line, size, 1, gains, *line_scratch[2:4], sum_send, sum_recv)
@@ -819,8 +801,6 @@
     da.second()
     gin.step(1)
     gin.step(2)
-    for copy in across[:1]:
-        copy.start()
     out_all.begin()
     gain_one = wout_ref[query_width : query_width + 1, :].astype(F32)
     grad_gain = jnp.zeros((1, x_ref.shape[1]), F32)
@@ -854,13 +834,9 @@
             jnp.where(row == 1, gain_two_ref[0:1, columns], 0.0),
         ).astype(BF16)
     gain.begin()
-    for copy in across[1:2]:
-        copy.start()
     gain.step(0)
     gain.step(1)
     gain.step(2)
-    for copy in across[2:]:
-        copy.start()
     out_all.relay()
     swap.wait_recv()
     for h in range(2):
@@ -901,12 +877,10 @@
     for item in last + (out_all, da, gin, gain):
         item.finish()
     swap.wait_send()
-    for copy in across:
-        copy.wait()
 
 
 def close_transfers(
-    da_part, e_own, e_total, x, middle, grad_middle, gain_two, w_out, grad_in, out_low, sent,
+    da_part, e_own, e_total, x, middle, grad_middle, gain_two, w_out, grad_in, out_low,
     query_width, collective_id,
 ):
     tokens, model_width = x.shape
@@ -918,7 +892,7 @@
     for shape in (grad_in.shape, (size,) + gain_shape):
         line_scratch += [pltpu.VMEM((2,) + shape, BF16)] * 2
     return pl.pallas_call(
-        functools.partial(close_kernel, size, query_width, len(sent)),
+        functools.partial(close_kernel, size, query_width),
         out_shape=[
             jax.ShapeDtypeStruct(wide, BF16),
             jax.ShapeDtypeStruct(wide, BF16),
@@ -926,10 +900,9 @@
             jax.ShapeDtypeStruct((8, out_rows, out_columns), BF16),
             jax.ShapeDtypeStruct((8,) + gain_shape, BF16),
             jax.ShapeDtypeStruct((8,) + note_shape, F32),
-        ]
-        + [jax.ShapeDtypeStruct(array.shape, array.dtype) for array in sent],
-        in_specs=in_vmem(10) + anywhere(len(sent)),
-        out_specs=in_vmem(2) + anywhere(4 + len(sent)),
+        ],
+        in_specs=in_vmem(10),
+        out_specs=in_vmem(2) + anywhere(4),
         scratch_shapes=[
             pltpu.VMEM(wide, BF16),
             pltpu.VMEM((size,) + gain_shape, BF16),
@@ -941,7 +914,7 @@
         ]
         + scatter_scratch(*wide, BF16)
         + line_scratch
-        + [pltpu.SemaphoreType.DMA((2, len(sent))), pltpu.SemaphoreType.DMA((2,))]
+        + [pltpu.SemaphoreType.DMA((2,))]
         + scatter_sems(1)
         + line_scatter_sems(2, size)
         + line_gather_sems(1, size)
@@ -949,7 +922,7 @@
         compiler_params=talk_params(collective_id),
         cost_estimate=pl.CostEstimate(flops=0, bytes_accessed=200_000_000, transcendentals=0),
         name="close_transfers",
-    )(da_part, e_own, e_total, x, middle, grad_middle, gain_two, w_out, grad_in, out_low, *sent)
+    )(da_part, e_own, e_total, x, middle, grad_middle, gain_two, w_out, grad_in, out_low)
 
 
 def dot(first, second, contract=(1, 0)):
@@ -1406,7 +1379,7 @@
         made = []
         for k in range(3):
             source = self.stages[k].at[e, (1, 0, 3)[hop]]
-            target = self.far[k] if hop == 2 else (self.nears, self.came)[hop][k].at[e]
+            target = self.far[3 * e + k] if hop == 2 else (self.nears, self.came)[hop][k].at[e]
             peer = self.across if hop == 2 else self.beside
             made.append(
                 push(source, target, self.sems.at[0, hop, k, e], self.sems.at[1, hop, k, e], "fsdp", peer)
@@ -1426,7 +1399,7 @@
 
     def finish(self, count):
         for e in range(count):
-            for hop in range(3 if e == 0 else 2):
+            for hop in range(3 if e < count - 1 else 2):
                 for copy in self.copies(e, hop):
                     copy.wait_send()
                     if hop:
@@ -1439,8 +1412,9 @@
     middle_ref, marked_ref, win_ref, wout_ref,
     out_hbm, dw_out, dl_out, grad_ref, gain_ref, *rest,
 ):
-    kept_hbm, came_hbm, far_hbm, rest = rest[0:3], rest[3:6], rest[6:9], rest[9:]
-    other_hbm, rest = rest[: 3 * (here - 1)], rest[3 * (here - 1) :]
+    kept_hbm, came_hbm, rest = rest[0:3], rest[3:6], rest[6:]
+    far_hbm, rest = rest[: 3 * (here - 1)], rest[3 * (here - 1) :]
+    other_hbm, rest = rest[:3], rest[3:]
     (
         b_ref, dy_ref, in_ref, down_ref, hidden_ref, back_ref, out_ref, db_ref, dg_ref,
         down_stage, gate_stage, up_stage, down_near, gate_near, up_near,
@@ -1627,14 +1601,16 @@
                     db_total[rows] = db_other.total(h).astype(BF16)
                 swap_g.start()
                 swap_b.start()
-                trade.send(here - 2, 1)
-                trade.send(here - 1, 0)
-                trade.send(here - 1, 1)
 
             @pl.when(last & (p == 2))
             def _():
                 dg.first()
                 db.first()
+                trade.add(here - 2)
+                trade.send(here - 2, 2)
+                trade.send(here - 2, 1)
+                trade.send(here - 1, 0)
+                trade.send(here - 1, 1)
 
             return carry
 
@@ -1651,17 +1627,6 @@
         store.start()
     dg.second()
     db.second()
-    others = []
-
-    def give_other(e):
-        trade.add(e)
-        for k, stage in enumerate((down_stage, gate_stage, up_stage)):
-            target = other_hbm[3 * (e - 1) + k]
-            others.append(pltpu.make_async_copy(stage.at[e, 3], target, other_sem.at[e - 1, k]))
-            others[-1].start()
-
-    for e in range(1, here - 1):
-        give_other(e)
     gain = wout_ref[query_width + 1 : query_width + 2, :].astype(F32)
     router = win_ref[:, router_at : router_at + LANES]
     gain_grad = jnp.zeros((1, model_width), F32)
@@ -1696,7 +1661,13 @@
     dl.relay()
     dw.relay_diagonal()
     dl.relay_diagonal()
-    give_other(here - 1)
+    trade.add(here - 1)
+    others = [
+        pltpu.make_async_copy(stage.at[here - 1, 3], other_hbm[k], other_sem.at[k])
+        for k, stage in enumerate((down_stage, gate_stage, up_stage))
+    ]
+    for copy in others:
+        copy.start()
     for item in (dg_other, db_other, dg, db, dw, dl):
         item.finish()
     swap_b.wait_send()
@@ -1759,7 +1730,7 @@
             pltpu.SemaphoreType.DMA((2, tiles)),
             pltpu.SemaphoreType.DMA((tiles,)),
             pltpu.SemaphoreType.DMA((3, here)),
-            pltpu.SemaphoreType.DMA((here - 1, 3)),
+            pltpu.SemaphoreType.DMA((3,)),
             pltpu.SemaphoreType.DMA((2, 3, 3, here)),
             pltpu.SemaphoreType.DMA((4,)),
         ]
@@ -1776,8 +1747,7 @@
         b_all.reshape(flat), dy_all.reshape(flat), g_all.reshape(rows_all, LANES),
         w_gate, w_up, w_down, middle, marked, w_in, w_out,
     )
-    others = [out[at : at + 3] for at in range(14, 11 + 3 * here, 3)]
-    return [out[0].reshape(b_all.shape), *out[1:5], out[5:8], out[8:11], out[11:14], others]
+    return [out[0].reshape(b_all.shape), *out[1:5], out[5:8], out[8:11], out[11:-3], out[-3:]]
 
 
 def rotary_tables(length):
@@ -1919,20 +1889,19 @@
             b_all, dy_all, g_all, w_gate, w_up, w_down, middle, marked, w_in, w_out_rows,
             lane_of, query_width, router_at, 2,
         )
-        early = [array for given in others[:-1] for array in given]
         da_part, grad_in, out_low, e_own, e_total, *crossed = attend_back(
             dw_all.reshape(length, model_width), w_in, w_out_rows, cosine, sine, saved,
             b_all.reshape(2 * length, model_width), dl_all.reshape(length, LANES), per_group,
-            (sum_part, early), 4,
-        )
-        outcome, grad_input, in_all, out_all, gains_all, notes_all, *crossed_last = close_transfers(
+            (sum_part, others), 4,
+        )
+        outcome, grad_input, in_all, out_all, gains_all, notes_all = close_transfers(
             da_part.reshape(wide), e_own, e_total, own_rows, middle, grad_middle, gain_two_grad,
-            w_out_rows, grad_in.reshape(lines, shard, in_width), out_low, others[-1],
+            w_out_rows, grad_in.reshape(lines, shard, in_width), out_low,
             query_width, 3,
         )
         squares = jnp.sum(notes_all, axis=0)[:5, 0]
         query, key, value, router_grad, proj, down, gate, up = finish(
-            in_all, out_all, kept, came, [*far, *crossed, *crossed_last], per_group, experts_all
+            in_all, out_all, kept, came, [*far, *crossed], per_group, experts_all
         )
         reduced = [gate, up, down]
         gain_rows = jnp.sum(gains_all[:, :2].astype(F32), axis=0)

time: 442 us -> 434 us (0.982)
  Pallas kernels: 423 us -> 415 us
    pallas_call x1, Pallas kernels: 96.3 us -> 75.7 us  [close_transfers(): pl.pallas_call(functools.partial(close_kernel, size, query_width), out_sh...]
    pallas_call x1, Pallas kernels: 125 us -> 139 us  [experts_back(): pl.pallas_call(functools.partial(experts_back_kernel, here, tile, lane_of...]
where the time goes in v1:
time: 434 us
  Pallas kernels  415 us (96%)
  local copies, waits for them, and re-layouts  10.8 us (2%)
  other arithmetic  7.05 us (2%)
    pallas_call x1, Pallas kernels, experts_back(): pl.pallas_call(functools.partial(experts_back_kernel, here, tile, lane_of...  139 us
    pallas_call x1, Pallas kernels, close_transfers(): pl.pallas_call(functools.partial(close_kernel, size, query_width), out_sh...  75.7 us
    pallas_call x1, Pallas kernels, middle_transfers(): pl.pallas_call(functools.partial(middle_kernel, query_width, router_at),...  66 us
    pallas_call x1, Pallas kernels, open_transfers(): pl.pallas_call(functools.partial(open_kernel, size), out_shape=[jax.Shape...  59 us
    pallas_call x1, Pallas kernels, attend_back(): pl.pallas_call(kernel, out_shape=shapes, in_specs=in_specs, out_specs=out...  50.6 us
    pallas_call x1, Pallas kernels, attend(): pl.pallas_call(functools.partial(attend_kernel, per_group), out_shape=sha...  15.8 us
    pallas_call x1, Pallas kernels, finish(): pl.pallas_call(functools.partial(finish_kernel, per_group, here), out_sha...  9.04 us

profile of v1, /device:TPU:0, one launch (start us, length us, event | category | flops | bytes accessed | tf_op | source)
XLA Modules:
  0.0 433.7 jit_solution(1887616854915512541)
XLA Ops:
  0.7 0.1 pad.3.clone
  0.7 0.7 broadcast_in_dim.20
  1.4 0.7 broadcast_in_dim.21
  2.1 0.8 copy.36
  2.9 0.3 compare_reduce_fusion
  3.2 0.6 convert_element_type.27.chosen_ref
  3.8 0.8 copy.35
  4.6 0.9 constant_dynamic-slice_fusion
  5.6 0.8 maximum_maximum_fusion.wout_ref
  6.3 1.1 constant_dynamic-slice_fusion.3
  7.4 1.1 constant_dynamic-slice_fusion.1
  8.5 0.9 concatenate.6.win_ref
  9.5 3.1 negate_select_fusion
  12.5 59.0 %open_transfers.1 = (bf16[8,128,1536]{2,1,0:T(8,128)(2,1)}, bf16[16,128,1536]{2,1,0:T(8,128)(2,1)}, bf16[1536,384]{1,0:T(8,128)(2,1)}, bf16[208,1536]{1,0:T(8,128)(2,1)}) custom-call(bf16[128,1536]{1,0:T(8,128)(2,1)} %bitcast.15, bf16[128,1536]{1,0:T(8,128)(2,1)} %bitcast.23, bf16[384,384]{1,0:T(8,128)(2,1)} %concatenate.6.win_ref, ...), custom_call_target="tpu_custom_call" | custom-call | bytes 120000000 | tf_op jit(solution)/shard_map/open_transfers/pallas_call | solution.py:671
  71.5 15.8 %attend.1 = (bf16[1024,1536]{1,0:T(8,128)(2,1)}, bf16[1024,1536]{1,0:T(8,128)(2,1)}, bf16[3,1024,64]{2,1,0:T(8,128)(2,1)}, bf16[1024,64]{1,0:T(8,128)(2,1)}, bf1...) custom-call(bf16[1024,1536]{1,0:T(8,128)(2,1)} %bitcast.28, ...), custom_call_target="tpu_custom_call" | custom-call | flops 8000000000 | bytes 16000000 | tf_op jit(solution)/shard_map/attend/pallas_call | solution.py:999
  87.3 66.0 %middle_transfers.1 = (bf16[16,128,1536]{2,1,0:T(8,128)(2,1)}, f32[16,128,128]{2,1,0:T(8,128)}, f32[128,1536]{1,0:T(8,128)}, f32[128,128]{1,0:T(8,128)}) custom-call(bf16[8,128,1536]{2,1,0:T(8,128)(2,1)} %bitcast.19, bf16[128,1536]{1,0:T(8,128)(2,1)} %bitcast.16, bf16[1536,384]{1,0:T(8,128)(2,1)} %get-tuple-element.71.w_in_ref.win_ref.refs_1_, ...), custom_call_target="tpu_custom_call" | custom-call | bytes 150000000 | tf_op jit(solution)/shard_map/middle_transfers/pallas_call | solution.py:749
  153.4 138.9 %experts_back.1 = (bf16[2048,1536]{1,0:T(8,128)(2,1)}, bf16[8,128,1536]{2,1,0:T(8,128)(2,1)}, bf16[8,128,128]{2,1,0:T(8,128)(2,1)}, f32[128,1536]{1,0:T(8,128)},...) custom-call(bf16[2048,1536]{1,0:T(8,128)(2,1)} %bitcast.25, ...), custom_call_target="tpu_custom_call" | custom-call | flops 43000000512 | bytes 42000000 | tf_op jit(solution)/shard_map/experts_back/pallas_call | solution.py:1693
  292.3 50.6 %attend_back.1 = (bf16[1024,1536]{1,0:T(8,128)(2,1)}, bf16[1536,384]{1,0:T(8,128)(2,1)}, bf16[192,384]{1,0:T(8,128)(2,1)}, f32[128,1536]{1,0:T(8,128)}, bf16[128...) custom-call(bf16[1024,1536]{1,0:T(8,128)(2,1)} %bitcast.31, ...), custom_call_target="tpu_custom_call" | custom-call | flops 20000000000 | bytes 30000000 | tf_op jit(solution)/shard_map/attend_back/pallas_call | solution.py:1180
  342.8 75.7 %close_transfers.1 = (bf16[128,1536]{1,0:T(8,128)(2,1)}, bf16[128,1536]{1,0:T(8,128)(2,1)}, bf16[8,384,384]{2,1,0:T(8,128)(2,1)}, bf16[8,192,384]{2,1,0:T(8,128)...) custom-call(bf16[8,128,1536]{2,1,0:T(8,128)(2,1)} %bitcast.18, f32[128,1536]{1,0:T(8,128)} %get-tuple-element.92.e_own, ...), custom_call_target="tpu_custom_call" | custom-call | bytes 200000000 | tf_op jit(solution)/shard_map/close_transfers/pallas_call | solution.py:894
  418.6 0.8 convert_reduce_fusion
  419.4 0.6 slice_reduce_fusion
  420.0 0.9 reduce_sum.19
  420.9 0.6 fusion.8
  421.5 0.0 copy-start.1
  421.5 0.0 copy-start
  421.5 9.0 %finish.1 = (f32[384,1536]{1,0:T(8,128)}, f32[384,512]{1,0:T(8,128)}, f32[384,512]{1,0:T(8,128)}, f32[384,24]{1,0:T(8,128)}, f32[1536,384]{1,0:T(8,128)}, /*inde...) custom-call(bf16[8,384,384]{2,1,0:T(8,128)(2,1)} %get-tuple-element.101.in_ref, ...), custom_call_target="tpu_custom_call" | custom-call | bytes 25000000 | tf_op jit(solution)/shard_map/finish/pallas_call | solution.py:1809
  430.5 1.6 copy.37
  432.2 0.0 copy-done.1
  432.2 0.7 copy.40
  432.9 0.0 copy-done
  432.9 0.7 copy.41
  (6 shorter events, 0.0 us)
Async XLA Ops:
  421.5 10.7 %copy-start.1 = (bf16[128,1536]{1,0:T(8,128)(2,1)S(1)}, bf16[128,1536]{1,0:T(8,128)(2,1)}, u32[]{:S(2)}) copy-start(bf16[128,1536]{1,0:T(8,128)(2,1)} %get-tuple-element.98) | copy-start | bytes 1179652
  421.5 11.4 %copy-start = (bf16[128,1536]{1,0:T(8,128)(2,1)S(1)}, bf16[128,1536]{1,0:T(8,128)(2,1)}, u32[]{:S(2)}) copy-start(bf16[128,1536]{1,0:T(8,128)(2,1)} %get-tuple-element.99) | copy-start | bytes 1179652

commit v2 on v1

--- a/solution.py
+++ b/solution.py
@@ -623,152 +623,6 @@
     return pltpu.CompilerParams(
         collective_id=collective_id, has_side_effects=True, vmem_limit_bytes=VMEM_LIMIT
     )
-
-
-def open_kernel(
-    size, x_ref, dy_ref, win_ref, wout_ref,
-    x_out, dy_out, win_out, wout_out,
-    landed, swap_sems, own_sem, send_sem, recv_sem, line_own, line_send, line_recv,
-):
-    plane, line = plane_neighbours(), lax.axis_index("fsdp")
-    meet(plane, line, size, True)
-    swap = push(dy_ref, landed, swap_sems.at[0], swap_sems.at[1], "fsdp", pair_of(line))
-    sems = (own_sem, send_sem, recv_sem)
-    line_sems = (line_own, line_send, line_recv)
-    x = Gather(plane, 0, x_ref, x_out, 0, *sems)
-    dy = Gather(plane, 1, dy_ref, dy_out, 0, *sems)
-    other = Gather(plane, 2, landed, dy_out, 8, *sems)
-    win = LineGather(line, size, 0, win_ref, win_out, 0, *line_sems)
-    wout = LineGather(line, size, 1, wout_ref, wout_out, 1, *line_sems)
-    win.begin()
-    x.begin()
-    swap.start()
-    wout.begin()
-    dy.begin()
-    x.relay()
-    win.step(0)
-    x.relay_diagonal()
-    wout.step(0)
-    win.step(1)
-    dy.relay()
-    swap.wait_recv()
-    other.begin()
-    wout.step(1)
-    dy.relay_diagonal()
-    win.step(2)
-    wout.step(2)
-    other.relay()
-    other.relay_diagonal()
-    for part in (x, dy, other, win, wout):
-        part.finish()
-    swap.wait_send()
-
-
-def open_transfers(x, dy, w_in_shard, w_out_shard, size, collective_id):
-    tokens, model_width = x.shape
-    rows, columns = w_in_shard.shape
-    out_rows, out_columns = w_out_shard.shape
-    return pl.pallas_call(
-        functools.partial(open_kernel, size),
-        out_shape=[
-            jax.ShapeDtypeStruct((8, tokens, model_width), BF16),
-            jax.ShapeDtypeStruct((16, tokens, model_width), BF16),
-            jax.ShapeDtypeStruct((rows * size, columns), BF16),
-            jax.ShapeDtypeStruct((out_rows, out_columns * size), BF16),
-        ],
-        in_specs=in_vmem(4),
-        out_specs=anywhere(4),
-        scratch_shapes=[pltpu.VMEM((tokens, model_width), BF16), pltpu.SemaphoreType.DMA((2,))]
-        + gather_sems(3)
-        + line_gather_sems(2, size),
-        compiler_params=talk_params(collective_id),
-        cost_estimate=pl.CostEstimate(flops=0, bytes_accessed=120_000_000, transcendentals=0),
-        name="open_transfers",
-    )(x, dy, w_in_shard, w_out_shard)
-
-
-def middle_kernel(
-    query_width, router_at, part_ref, x_ref, win_ref, wout_ref, chosen_ref,
-    b_out, g_out, middle_ref, marked_ref,
-    routed, b_landed, g_landed, *rest,
-):
-    scratch, rest = rest[:6], rest[6:]
-    swap_sems, scatter_send, scatter_recv, own_sem, send_sem, recv_sem = rest
-    plane, line = plane_neighbours(), lax.axis_index("fsdp")
-    meet(plane, line, 4, False)
-    scatter = Scatter(plane, 0, part_ref, 0, scratch, scatter_send, scatter_recv)
-    scatter.begin()
-    scatter.first()
-    scatter.second()
-    half = x_ref.shape[0] // 2
-    gain = wout_ref[query_width + 1 : query_width + 2, :].astype(F32)
-    router = win_ref[:, router_at : router_at + LANES]
-    for h in range(2):
-        rows = pl.ds(h * half, half)
-        middle = x_ref[rows].astype(F32) + RESIDUAL_SCALE * scatter.total(h)
-        middle_ref[rows] = middle
-        inverse = lax.rsqrt(jnp.mean(middle * middle, axis=1, keepdims=True) + EPSILON)
-        b = (middle * inverse * gain).astype(BF16)
-        routed[rows] = b
-        chosen = chosen_ref[rows] > 0.0
-        logits = jnp.where(chosen, dot(b, router), -1e30)
-        lifted = jnp.where(chosen, jnp.exp(logits - jnp.max(logits, axis=1, keepdims=True)), 0.0)
-        gates = lifted / jnp.sum(lifted, axis=1, keepdims=True)
-        marked_ref[rows] = jnp.where(chosen, gates, -1.0)
-    swap_b = push(routed, b_landed, swap_sems.at[0], swap_sems.at[1], "fsdp", pair_of(line))
-    swap_g = push(marked_ref, g_landed, swap_sems.at[2], swap_sems.at[3], "fsdp", pair_of(line))
-    swap_b.start()
-    swap_g.start()
-    sems = (own_sem, send_sem, recv_sem)
-    b = Gather(plane, 0, routed, b_out, 0, *sems)
-    g = Gather(plane, 1, marked_ref, g_out, 0, *sems)
-    b_other = Gather(plane, 2, b_landed, b_out, 8, *sems)
-    g_other = Gather(plane, 3, g_landed, g_out, 8, *sems)
-    b.begin()
-    g.begin()
-    b.relay()
-    g.relay()
-    b.relay_diagonal()
-    g.relay_diagonal()
-    swap_b.wait_recv()
-    swap_g.wait_recv()
-    b_other.begin()
-    g_other.begin()
-    b_other.relay()
-    g_other.relay()
-    b_other.relay_diagonal()
-    g_other.relay_diagonal()
-    for item in (b, g, b_other, g_other, scatter):
-        item.finish()
-    swap_b.wait_send()
-    swap_g.wait_send()
-
-
-def middle_transfers(part, x, w_in, w_out, chosen, query_width, router_at, collective_id):
-    tokens, model_width = x.shape
-    return pl.pallas_call(
-        functools.partial(middle_kernel, query_width, router_at),
-        out_shape=[
-            jax.ShapeDtypeStruct((16, tokens, model_width), BF16),
-            jax.ShapeDtypeStruct((16, tokens, LANES), F32),
-            jax.ShapeDtypeStruct((tokens, model_width), F32),
-            jax.ShapeDtypeStruct((tokens, LANES), F32),
-        ],
-        in_specs=in_vmem(5),
-        out_specs=anywhere(2) + in_vmem(2),
-        scratch_shapes=[
-            pltpu.VMEM((tokens, model_width), BF16),
-            pltpu.VMEM((tokens, model_width), BF16),
-            pltpu.VMEM((tokens, LANES), F32),
-        ]
-        + scatter_scratch(tokens, model_width, BF16)
-        + [pltpu.SemaphoreType.DMA((4,))]
-        + scatter_sems(1)
-        + gather_sems(4),
-        compiler_params=talk_params(collective_id),
-        cost_estimate=pl.CostEstimate(flops=0, bytes_accessed=150_000_000, transcendentals=0),
-        name="middle_transfers",
-    )(part, x, w_in, w_out, chosen)
 
 
 def close_kernel(
@@ -944,18 +798,30 @@
     return values * cosine + swapped * sine
 
 
-def attend_kernel(
-    per_group, x_ref, w_in_ref, w_out_ref, cos_ref, sin_ref,
-    part_ref, a_ref, q_ref, k_ref, v_ref, o_ref, lse_ref,
+def attend_kernel(per_group, x_ref, w_in_ref, w_out_ref, cos_ref, sin_ref, part_ref, *outs):
+    def take(rows):
+        return x_ref[rows, :]
+
+    def put(i, part):
+        part_ref[i * BLOCK : (i + 1) * BLOCK, :] = part
+
+    attend_steps(
+        per_group, x_ref.shape[0], take, put, lambda step: None, w_in_ref, w_out_ref, cos_ref,
+        sin_ref, *outs,
+    )
+
+
+def attend_steps(
+    per_group, length, take, put, hook, w_in_ref, w_out_ref, cos_ref, sin_ref,
+    a_ref, q_ref, k_ref, v_ref, o_ref, lse_ref,
 ):
-    length, model_width = x_ref.shape
     query_width = per_group * HEAD_DIM
     turned = query_width + HEAD_DIM
     gain = w_out_ref[query_width : query_width + 1, :].astype(F32)
 
     def project(i, carry):
         rows = pl.ds(pl.multiple_of(i * BLOCK, BLOCK), BLOCK)
-        x = x_ref[rows, :].astype(F32)
+        x = take(rows).astype(F32)
         inverse = lax.rsqrt(jnp.mean(x * x, axis=1, keepdims=True) + EPSILON)
         a = (x * inverse * gain).astype(BF16)
         a_ref[rows, :] = a
@@ -968,6 +834,7 @@
         return carry
 
     lax.fori_loop(0, length // BLOCK, project, 0)
+    hook(0)
     for i in range(length // BLOCK):
         seen = (i + 1) * BLOCK
         rows = slice(i * BLOCK, seen)
@@ -981,21 +848,181 @@
             mixed = dot(weights, values)
             o_ref[rows, h * HEAD_DIM : (h + 1) * HEAD_DIM] = mixed.astype(BF16)
             lse_ref[h, rows, :] = peak + jnp.log(total)
-        part_ref[rows, :] = dot(o_ref[rows, :], w_out_ref[:query_width, :]).astype(BF16)
-
-
-def attend(x_all, w_in, w_out, cosine, sine, per_group):
-    length, model_width = x_all.shape
-    query_width = per_group * HEAD_DIM
-    shapes = [
-        jax.ShapeDtypeStruct((length, model_width), BF16),
+        put(i, dot(o_ref[rows, :], w_out_ref[:query_width, :]).astype(BF16))
+        hook(1 + i)
+
+
+def saved_shapes(length, model_width, per_group):
+    return [
         jax.ShapeDtypeStruct((length, model_width), BF16),
         jax.ShapeDtypeStruct((per_group, length, HEAD_DIM), BF16),
         jax.ShapeDtypeStruct((length, HEAD_DIM), BF16),
         jax.ShapeDtypeStruct((length, HEAD_DIM), BF16),
-        jax.ShapeDtypeStruct((length, query_width), BF16),
+        jax.ShapeDtypeStruct((length, per_group * HEAD_DIM), BF16),
         jax.ShapeDtypeStruct((per_group, length, 1), F32),
     ]
+
+
+def front_kernel(
+    size, per_group, router_at, x_ref, dy_ref, win_shard, wout_shard, chosen_ref, cos_ref, sin_ref,
+    dy_out, win_ref, wout_ref, *rest,
+):
+    saved, rest = rest[:6], rest[6:]
+    b_out, g_out, middle_ref, marked_ref, *rest = rest
+    x_all, part_ref, dy_landed, routed, b_landed, g_landed, *rest = rest
+    scratch, rest = rest[:5], rest[5:]
+    (
+        swap_sems, scatter_send, scatter_recv, own_sem, send_sem, recv_sem,
+        line_own, line_send, line_recv,
+    ) = rest
+    plane, line = plane_neighbours(), lax.axis_index("fsdp")
+    pair = pair_of(line)
+    tokens = x_ref.shape[0]
+    half, per_block = tokens // 2, BLOCK // tokens
+    query_width = per_group * HEAD_DIM
+    meet(plane, line, size, True)
+    sems = (own_sem, send_sem, recv_sem)
+    line_sems = (line_own, line_send, line_recv)
+    x = Gather(plane, 0, x_ref, x_all, 0, *sems)
+    dy = Gather(plane, 1, dy_ref, dy_out, 0, *sems)
+    other = Gather(plane, 2, dy_landed, dy_out, 8, *sems)
+    win = LineGather(line, size, 0, win_shard, win_ref, 0, *line_sems)
+    wout = LineGather(line, size, 1, wout_shard, wout_ref, 1, *line_sems)
+    scatter = Scatter(plane, 0, part_ref, 0, scratch, scatter_send, scatter_recv)
+    swap_dy = push(dy_ref, dy_landed, swap_sems.at[0], swap_sems.at[1], "fsdp", pair)
+    swap_b = push(routed, b_landed, swap_sems.at[2], swap_sems.at[3], "fsdp", pair)
+    swap_g = push(marked_ref, g_landed, swap_sems.at[4], swap_sems.at[5], "fsdp", pair)
+    win.begin()
+    x.begin()
+    wout.begin()
+    x.relay()
+    win.step(0)
+    x.relay_diagonal()
+    wout.step(0)
+    dy.begin()
+    win.step(1)
+    swap_dy.start()
+    wout.step(1)
+    win.step(2)
+    wout.step(2)
+    for item in (x, win, wout):
+        item.finish()
+
+    def take(rows):
+        block = pl.ds(rows.start // tokens, per_block)
+        return x_all[block].reshape(BLOCK, x_all.shape[2])
+
+    def put(i, part):
+        for t in range(per_block):
+            part_ref[per_block * i + t] = part[t * tokens : (t + 1) * tokens]
+
+    def hook(step):
+        if step == 0:
+            dy.relay()
+        elif step == 2:
+            dy.relay_diagonal()
+        elif step == 3:
+            swap_dy.wait_recv()
+            other.begin()
+
+    attend_steps(
+        per_group, x_all.shape[0] * tokens, take, put, hook, win_ref, wout_ref, cos_ref, sin_ref,
+        *saved,
+    )
+    scatter.begin()
+    scatter.first()
+    other.relay()
+    scatter.second()
+    gain = wout_ref[query_width + 1 : query_width + 2, :].astype(F32)
+    router = win_ref[:, router_at : router_at + LANES]
+    for h in range(2):
+        rows = pl.ds(h * half, half)
+        middle = x_ref[rows].astype(F32) + RESIDUAL_SCALE * scatter.total(h)
+        middle_ref[rows] = middle
+        inverse = lax.rsqrt(jnp.mean(middle * middle, axis=1, keepdims=True) + EPSILON)
+        b = (middle * inverse * gain).astype(BF16)
+        routed[rows] = b
+        chosen = chosen_ref[rows] > 0.0
+        logits = jnp.where(chosen, dot(b, router), -1e30)
+        lifted = jnp.where(chosen, jnp.exp(logits - jnp.max(logits, axis=1, keepdims=True)), 0.0)
+        gates = lifted / jnp.sum(lifted, axis=1, keepdims=True)
+        marked_ref[rows] = jnp.where(chosen, gates, -1.0)
+    swap_b.start()
+    swap_g.start()
+    b = Gather(plane, 3, routed, b_out, 0, *sems)
+    g = Gather(plane, 4, marked_ref, g_out, 0, *sems)
+    b_other = Gather(plane, 5, b_landed, b_out, 8, *sems)
+    g_other = Gather(plane, 6, g_landed, g_out, 8, *sems)
+    b.begin()
+    g.begin()
+    other.relay_diagonal()
+    b.relay()
+    g.relay()
+    b.relay_diagonal()
+    g.relay_diagonal()
+    swap_b.wait_recv()
+    swap_g.wait_recv()
+    b_other.begin()
+    g_other.begin()
+    b_other.relay()
+    g_other.relay()
+    b_other.relay_diagonal()
+    g_other.relay_diagonal()
+    for item in (dy, other, b, g, b_other, g_other, scatter):
+        item.finish()
+    for swap in (swap_dy, swap_b, swap_g):
+        swap.wait_send()
+
+
+def front(
+    x, dy, w_in_shard, w_out_shard, chosen, cosine, sine, size, per_group, router_at, collective_id
+):
+    tokens, model_width = x.shape
+    rows, columns = w_in_shard.shape
+    out_rows, out_columns = w_out_shard.shape
+    wide, narrow = (tokens, model_width), (tokens, LANES)
+    out = pl.pallas_call(
+        functools.partial(front_kernel, size, per_group, router_at),
+        out_shape=[
+            jax.ShapeDtypeStruct((16,) + wide, BF16),
+            jax.ShapeDtypeStruct((rows * size, columns), BF16),
+            jax.ShapeDtypeStruct((out_rows, out_columns * size), BF16),
+        ]
+        + saved_shapes(8 * tokens, model_width, per_group)
+        + [
+            jax.ShapeDtypeStruct((16,) + wide, BF16),
+            jax.ShapeDtypeStruct((16,) + narrow, F32),
+            jax.ShapeDtypeStruct(wide, F32),
+            jax.ShapeDtypeStruct(narrow, F32),
+        ],
+        in_specs=in_vmem(7),
+        out_specs=anywhere(1) + in_vmem(8) + anywhere(2) + in_vmem(2),
+        scratch_shapes=[
+            pltpu.VMEM((8,) + wide, BF16),
+            pltpu.VMEM((8,) + wide, BF16),
+            pltpu.VMEM(wide, BF16),
+            pltpu.VMEM(wide, BF16),
+            pltpu.VMEM(wide, BF16),
+            pltpu.VMEM(narrow, F32),
+        ]
+        + scatter_scratch(*wide, BF16, True)
+        + [pltpu.SemaphoreType.DMA((6,))]
+        + scatter_sems(1)
+        + gather_sems(7)
+        + line_gather_sems(2, size),
+        compiler_params=talk_params(collective_id),
+        cost_estimate=pl.CostEstimate(
+            flops=8_000_000_000, bytes_accessed=150_000_000, transcendentals=2_000_000
+        ),
+        name="front",
+    )(x, dy, w_in_shard, w_out_shard, chosen, cosine, sine)
+    return [*out[:3], out[3:9], *out[9:]]
+
+
+def attend(x_all, w_in, w_out, cosine, sine, per_group):
+    length, model_width = x_all.shape
+    shapes = [jax.ShapeDtypeStruct((length, model_width), BF16)]
+    shapes += saved_shapes(length, model_width, per_group)
     return pl.pallas_call(
         functools.partial(attend_kernel, per_group),
         out_shape=shapes,
@@ -1869,43 +1896,39 @@
     wide = (peers, tokens, model_width)
 
     if paired:
-        x_all, dy_all, w_in, w_out_rows = open_transfers(
-            own_rows, own_grad, w_in_shard, w_out_shard, lines, 0
-        )
+        dy_all, w_in, w_out_rows, saved, b_all, g_all, middle, marked = front(
+            own_rows, own_grad, w_in_shard, w_out_shard, chosen, cosine, sine, lines, per_group,
+            router_at, 0,
+        )
+        sum_part, dw_all, dl_all, grad_middle, gain_two_grad, kept, came, far, others = experts_back(
+            b_all, dy_all, g_all, w_gate, w_up, w_down, middle, marked, w_in, w_out_rows,
+            lane_of, query_width, router_at, 2,
+        )
+        da_part, grad_in, out_low, e_own, e_total, *crossed = attend_back(
+            dw_all.reshape(length, model_width), w_in, w_out_rows, cosine, sine, saved,
+            b_all.reshape(2 * length, model_width), dl_all.reshape(length, LANES), per_group,
+            (sum_part, others), 4,
+        )
+        outcome, grad_input, in_all, out_all, gains_all, notes_all = close_transfers(
+            da_part.reshape(wide), e_own, e_total, own_rows, middle, grad_middle, gain_two_grad,
+            w_out_rows, grad_in.reshape(lines, shard, in_width), out_low,
+            query_width, 3,
+        )
+        squares = jnp.sum(notes_all, axis=0)[:5, 0]
+        query, key, value, router_grad, proj, down, gate, up = finish(
+            in_all, out_all, kept, came, [*far, *crossed], per_group, experts_all
+        )
+        reduced = [gate, up, down]
+        gain_rows = jnp.sum(gains_all[:, :2].astype(F32), axis=0)
     else:
         x_all, dy_all = plane_gather([own_rows, own_grad], 0)
         w_in, w_out_rows = (
             lax.all_gather(w_in_shard, "fsdp", axis=0, tiled=True),
             lax.all_gather(w_out_shard, "fsdp", axis=1, tiled=True),
         )
-    part, *saved = attend(
-        x_all.reshape(length, model_width), w_in, w_out_rows, cosine, sine, per_group
-    )
-    if paired:
-        b_all, g_all, middle, marked = middle_transfers(
-            part.reshape(wide), own_rows, w_in, w_out_rows, chosen, query_width, router_at, 1
-        )
-        sum_part, dw_all, dl_all, grad_middle, gain_two_grad, kept, came, far, others = experts_back(
-            b_all, dy_all, g_all, w_gate, w_up, w_down, middle, marked, w_in, w_out_rows,
-            lane_of, query_width, router_at, 2,
-        )
-        da_part, grad_in, out_low, e_own, e_total, *crossed = attend_back(
-            dw_all.reshape(length, model_width), w_in, w_out_rows, cosine, sine, saved,
-            b_all.reshape(2 * length, model_width), dl_all.reshape(length, LANES), per_group,
-            (sum_part, others), 4,
-        )
-        outcome, grad_input, in_all, out_all, gains_all, notes_all = close_transfers(
-            da_part.reshape(wide), e_own, e_total, own_rows, middle, grad_middle, gain_two_grad,
-            w_out_rows, grad_in.reshape(lines, shard, in_width), out_low,
-            query_width, 3,
-        )
-        squares = jnp.sum(notes_all, axis=0)[:5, 0]
-        query, key, value, router_grad, proj, down, gate, up = finish(
-            in_all, out_all, kept, came, [*far, *crossed], per_group, experts_all
-        )
-        reduced = [gate, up, down]
-        gain_rows = jnp.sum(gains_all[:, :2].astype(F32), axis=0)
-    else:
+        part, *saved = attend(
+            x_all.reshape(length, model_width), w_in, w_out_rows, cosine, sine, per_group
+        )
         (branch,) = plane_scatter([part.reshape(wide)], 1)
         gain_one = w_out_rows[query_width][None].astype(F32)
         gain_two = w_out_rows[query_width + 1][None].astype(F32)

time: 434 us -> 419 us (0.965)
  Pallas kernels: 415 us -> 400 us
    pallas_call x3 -> x1, Pallas kernels: 141 us -> 130 us  [front(): pl.pallas_call(functools.partial(front_kernel, size, per_group, router_at...]
    pallas_call x1, Pallas kernels: 75.7 us -> 70.4 us  [close_transfers(): pl.pallas_call(functools.partial(close_kernel, size, query_width), out_sh...]
where the time goes in v2:
time: 419 us
  Pallas kernels  400 us (95%)
  local copies, waits for them, and re-layouts  10.8 us (3%)
  other arithmetic  7.05 us (2%)
    pallas_call x1, Pallas kernels, experts_back(): pl.pallas_call(functools.partial(experts_back_kernel, here, tile, lane_of...  141 us
    pallas_call x1, Pallas kernels, front(): pl.pallas_call(functools.partial(front_kernel, size, per_group, router_at...  130 us
    pallas_call x1, Pallas kernels, close_transfers(): pl.pallas_call(functools.partial(close_kernel, size, query_width), out_sh...  70.4 us
    pallas_call x1, Pallas kernels, attend_back(): pl.pallas_call(kernel, out_shape=shapes, in_specs=in_specs, out_specs=out...  50.4 us
    pallas_call x1, Pallas kernels, finish(): pl.pallas_call(functools.partial(finish_kernel, per_group, here), out_sha...  9.04 us

profile of v2, /device:TPU:0, one launch (start us, length us, event | category | flops | bytes accessed | tf_op | source)
XLA Modules:
  0.0 418.8 jit_solution(16257927394816491212)
XLA Ops:
  0.7 0.1 pad.3.clone
  0.7 0.7 broadcast_in_dim.20
  1.4 0.7 broadcast_in_dim.21
  2.1 0.8 copy.36
  2.9 0.3 compare_reduce_fusion
  3.2 0.6 convert_element_type.25.chosen_ref
  3.8 0.8 copy.35
  4.6 0.9 constant_dynamic-slice_fusion
  5.6 0.8 maximum_maximum_fusion.wout_shard
  6.3 1.1 constant_dynamic-slice_fusion.3
  7.4 1.1 constant_dynamic-slice_fusion.1
  8.5 0.9 concatenate.6.win_shard
  9.5 3.1 negate_select_fusion
  12.5 129.7 %front.1 = (bf16[16,128,1536]{2,1,0:T(8,128)(2,1)}, bf16[1536,384]{1,0:T(8,128)(2,1)}, bf16[208,1536]{1,0:T(8,128)(2,1)}, bf16[1024,1536]{1,0:T(8,128)(2,1)}, bf...) custom-call(bf16[128,1536]{1,0:T(8,128)(2,1)} %bitcast.15, ...), custom_call_target="tpu_custom_call" | custom-call | flops 8000000000 | bytes 150000000 | tf_op jit(solution)/shard_map/front/pallas_call | solution.py:984
  142.2 140.6 %experts_back.1 = (bf16[2048,1536]{1,0:T(8,128)(2,1)}, bf16[8,128,1536]{2,1,0:T(8,128)(2,1)}, bf16[8,128,128]{2,1,0:T(8,128)(2,1)}, f32[128,1536]{1,0:T(8,128)},...) custom-call(bf16[2048,1536]{1,0:T(8,128)(2,1)} %bitcast.21, ...), custom_call_target="tpu_custom_call" | custom-call | flops 43000000512 | bytes 42000000 | tf_op jit(solution)/shard_map/experts_back/pallas_call | solution.py:1720
  282.8 50.4 %attend_back.1 = (bf16[1024,1536]{1,0:T(8,128)(2,1)}, bf16[1536,384]{1,0:T(8,128)(2,1)}, bf16[192,384]{1,0:T(8,128)(2,1)}, f32[128,1536]{1,0:T(8,128)}, bf16[128...) custom-call(bf16[1024,1536]{1,0:T(8,128)(2,1)} %bitcast.25, ...), custom_call_target="tpu_custom_call" | custom-call | flops 20000000000 | bytes 30000000 | tf_op jit(solution)/shard_map/attend_back/pallas_call | solution.py:1207
  333.3 70.4 %close_transfers.1 = (bf16[128,1536]{1,0:T(8,128)(2,1)}, bf16[128,1536]{1,0:T(8,128)(2,1)}, bf16[8,384,384]{2,1,0:T(8,128)(2,1)}, bf16[8,192,384]{2,1,0:T(8,128)...) custom-call(bf16[8,128,1536]{2,1,0:T(8,128)(2,1)} %bitcast.13, f32[128,1536]{1,0:T(8,128)} %get-tuple-element.88.e_own, ...), custom_call_target="tpu_custom_call" | custom-call | bytes 200000000 | tf_op jit(solution)/shard_map/close_transfers/pallas_call | solution.py:748
  403.7 0.8 convert_reduce_fusion
  404.5 0.6 slice_reduce_fusion
  405.1 0.9 reduce_sum.19
  405.9 0.6 fusion.8
  406.6 0.0 copy-start.1
  406.6 0.0 copy-start
  406.6 9.0 %finish.1 = (f32[384,1536]{1,0:T(8,128)}, f32[384,512]{1,0:T(8,128)}, f32[384,512]{1,0:T(8,128)}, f32[384,24]{1,0:T(8,128)}, f32[1536,384]{1,0:T(8,128)}, /*inde...) custom-call(bf16[8,384,384]{2,1,0:T(8,128)(2,1)} %get-tuple-element.97.in_ref, ...), custom_call_target="tpu_custom_call" | custom-call | bytes 25000000 | tf_op jit(solution)/shard_map/finish/pallas_call | solution.py:1836
  415.6 1.6 copy.37
  417.3 0.0 copy-done.1
  417.3 0.7 copy.40
  418.0 0.0 copy-done
  418.0 0.7 copy.41
  (6 shorter events, 0.0 us)
Async XLA Ops:
  406.6 10.7 %copy-start.1 = (bf16[128,1536]{1,0:T(8,128)(2,1)S(1)}, bf16[128,1536]{1,0:T(8,128)(2,1)}, u32[]{:S(2)}) copy-start(bf16[128,1536]{1,0:T(8,128)(2,1)} %get-tuple-element.94) | copy-start | bytes 1179652
  406.6 11.4 %copy-start = (bf16[128,1536]{1,0:T(8,128)(2,1)S(1)}, bf16[128,1536]{1,0:T(8,128)(2,1)}, u32[]{:S(2)}) copy-start(bf16[128,1536]{1,0:T(8,128)(2,1)} %get-tuple-element.95) | copy-start | bytes 1179652

commit v3 on v2

--- a/solution.py
+++ b/solution.py
@@ -901,10 +901,10 @@
     wout.step(0)
     dy.begin()
     win.step(1)
-    swap_dy.start()
     wout.step(1)
     win.step(2)
     wout.step(2)
+    swap_dy.start()
     for item in (x, win, wout):
         item.finish()
 
@@ -923,7 +923,6 @@
             dy.relay_diagonal()
         elif step == 3:
             swap_dy.wait_recv()
-            other.begin()
 
     attend_steps(
         per_group, x_all.shape[0] * tokens, take, put, hook, win_ref, wout_ref, cos_ref, sin_ref,
@@ -931,7 +930,6 @@
     )
     scatter.begin()
     scatter.first()
-    other.relay()
     scatter.second()
     gain = wout_ref[query_width + 1 : query_width + 2, :].astype(F32)
     router = win_ref[:, router_at : router_at + LANES]
@@ -955,15 +953,17 @@
     g_other = Gather(plane, 6, g_landed, g_out, 8, *sems)
     b.begin()
     g.begin()
-    other.relay_diagonal()
     b.relay()
     g.relay()
+    other.begin()
     b.relay_diagonal()
     g.relay_diagonal()
+    other.relay()
     swap_b.wait_recv()
     swap_g.wait_recv()
     b_other.begin()
     g_other.begin()
+    other.relay_diagonal()
     b_other.relay()
     g_other.relay()
     b_other.relay_diagonal()

time: 419 us -> 415 us (level)
  no operation moved by 1% of the time
where the time goes in v3:
time: 415 us
  Pallas kernels  396 us (95%)
  local copies, waits for them, and re-layouts  10.8 us (3%)
  other arithmetic  7.05 us (2%)
    pallas_call x1, Pallas kernels, experts_back(): pl.pallas_call(functools.partial(experts_back_kernel, here, tile, lane_of...  140 us
    pallas_call x1, Pallas kernels, front(): pl.pallas_call(functools.partial(front_kernel, size, per_group, router_at...  127 us
    pallas_call x1, Pallas kernels, close_transfers(): pl.pallas_call(functools.partial(close_kernel, size, query_width), out_sh...  70.4 us
    pallas_call x1, Pallas kernels, attend_back(): pl.pallas_call(kernel, out_shape=shapes, in_specs=in_specs, out_specs=out...  50.3 us
    pallas_call x1, Pallas kernels, finish(): pl.pallas_call(functools.partial(finish_kernel, per_group, here), out_sha...  9.04 us

profile of v3, /device:TPU:0, one launch (start us, length us, event | category | flops | bytes accessed | tf_op | source)
XLA Modules:
  0.0 414.8 jit_solution(7080556358324273037)
XLA Ops:
  0.7 0.1 pad.3.clone
  0.7 0.7 broadcast_in_dim.20
  1.4 0.7 broadcast_in_dim.21
  2.1 0.8 copy.36
  2.9 0.3 compare_reduce_fusion
  3.2 0.6 convert_element_type.25.chosen_ref
  3.8 0.8 copy.35
  4.6 0.9 constant_dynamic-slice_fusion
  5.6 0.8 maximum_maximum_fusion.wout_shard
  6.3 1.1 constant_dynamic-slice_fusion.3
  7.4 1.1 constant_dynamic-slice_fusion.1
  8.5 0.9 concatenate.6.win_shard
  9.5 3.1 negate_select_fusion
  12.5 126.6 %front.1 = (bf16[16,128,1536]{2,1,0:T(8,128)(2,1)}, bf16[1536,384]{1,0:T(8,128)(2,1)}, bf16[208,1536]{1,0:T(8,128)(2,1)}, bf16[1024,1536]{1,0:T(8,128)(2,1)}, bf...) custom-call(bf16[128,1536]{1,0:T(8,128)(2,1)} %bitcast.15, ...), custom_call_target="tpu_custom_call" | custom-call | flops 8000000000 | bytes 150000000 | tf_op jit(solution)/shard_map/front/pallas_call | solution.py:984
  139.1 140.0 %experts_back.1 = (bf16[2048,1536]{1,0:T(8,128)(2,1)}, bf16[8,128,1536]{2,1,0:T(8,128)(2,1)}, bf16[8,128,128]{2,1,0:T(8,128)(2,1)}, f32[128,1536]{1,0:T(8,128)},...) custom-call(bf16[2048,1536]{1,0:T(8,128)(2,1)} %bitcast.21, ...), custom_call_target="tpu_custom_call" | custom-call | flops 43000000512 | bytes 42000000 | tf_op jit(solution)/shard_map/experts_back/pallas_call | solution.py:1720
  279.1 50.3 %attend_back.1 = (bf16[1024,1536]{1,0:T(8,128)(2,1)}, bf16[1536,384]{1,0:T(8,128)(2,1)}, bf16[192,384]{1,0:T(8,128)(2,1)}, f32[128,1536]{1,0:T(8,128)}, bf16[128...) custom-call(bf16[1024,1536]{1,0:T(8,128)(2,1)} %bitcast.25, ...), custom_call_target="tpu_custom_call" | custom-call | flops 20000000000 | bytes 30000000 | tf_op jit(solution)/shard_map/attend_back/pallas_call | solution.py:1207
  329.4 70.4 %close_transfers.1 = (bf16[128,1536]{1,0:T(8,128)(2,1)}, bf16[128,1536]{1,0:T(8,128)(2,1)}, bf16[8,384,384]{2,1,0:T(8,128)(2,1)}, bf16[8,192,384]{2,1,0:T(8,128)...) custom-call(bf16[8,128,1536]{2,1,0:T(8,128)(2,1)} %bitcast.13, f32[128,1536]{1,0:T(8,128)} %get-tuple-element.88.e_own, ...), custom_call_target="tpu_custom_call" | custom-call | bytes 200000000 | tf_op jit(solution)/shard_map/close_transfers/pallas_call | solution.py:748
  399.7 0.8 convert_reduce_fusion
  400.6 0.6 slice_reduce_fusion
  401.2 0.9 reduce_sum.19
  402.0 0.6 fusion.8
  402.7 0.0 copy-start.1
  402.7 0.0 copy-start
  402.7 9.0 %finish.1 = (f32[384,1536]{1,0:T(8,128)}, f32[384,512]{1,0:T(8,128)}, f32[384,512]{1,0:T(8,128)}, f32[384,24]{1,0:T(8,128)}, f32[1536,384]{1,0:T(8,128)}, /*inde...) custom-call(bf16[8,384,384]{2,1,0:T(8,128)(2,1)} %get-tuple-element.97.in_ref, ...), custom_call_target="tpu_custom_call" | custom-call | bytes 25000000 | tf_op jit(solution)/shard_map/finish/pallas_call | solution.py:1836
  411.7 1.6 copy.37
  413.4 0.0 copy-done.1
  413.4 0.7 copy.40
  414.1 0.0 copy-done
  414.1 0.7 copy.41
  (6 shorter events, 0.0 us)
Async XLA Ops:
  402.7 10.7 %copy-start.1 = (bf16[128,1536]{1,0:T(8,128)(2,1)S(1)}, bf16[128,1536]{1,0:T(8,128)(2,1)}, u32[]{:S(2)}) copy-start(bf16[128,1536]{1,0:T(8,128)(2,1)} %get-tuple-element.94) | copy-start | bytes 1179652
  402.7 11.4 %copy-start = (bf16[128,1536]{1,0:T(8,128)(2,1)S(1)}, bf16[128,1536]{1,0:T(8,128)(2,1)}, u32[]{:S(2)}) copy-start(bf16[128,1536]{1,0:T(8,128)(2,1)} %get-tuple-element.95) | copy-start | bytes 1179652

commit v4 on v3

--- a/solution.py
+++ b/solution.py
@@ -648,10 +648,10 @@
     out_all = Gather(plane, 1, out_low, out_out, 0, *gathers)
     half = x_ref.shape[0] // 2
     gin.begin()
+    swap.start()
     da.begin()
     da.first()
     gin.step(0)
-    swap.start()
     da.second()
     gin.step(1)
     gin.step(2)

time: 415 us -> 417 us (level)
  no operation moved by 1% of the time
where the time goes in v4:
time: 417 us
  Pallas kernels  398 us (95%)
  local copies, waits for them, and re-layouts  10.8 us (3%)
  other arithmetic  7.05 us (2%)
    pallas_call x1, Pallas kernels, experts_back(): pl.pallas_call(functools.partial(experts_back_kernel, here, tile, lane_of...  140 us
    pallas_call x1, Pallas kernels, front(): pl.pallas_call(functools.partial(front_kernel, size, per_group, router_at...  127 us
    pallas_call x1, Pallas kernels, close_transfers(): pl.pallas_call(functools.partial(close_kernel, size, query_width), out_sh...  72.3 us
    pallas_call x1, Pallas kernels, attend_back(): pl.pallas_call(kernel, out_shape=shapes, in_specs=in_specs, out_specs=out...  50.3 us
    pallas_call x1, Pallas kernels, finish(): pl.pallas_call(functools.partial(finish_kernel, per_group, here), out_sha...  9.04 us

profile of v4, /device:TPU:0, one launch (start us, length us, event | category | flops | bytes accessed | tf_op | source)
XLA Modules:
  0.0 416.7 jit_solution(9914644728640742168)
XLA Ops:
  0.7 0.1 pad.3.clone
  0.7 0.7 broadcast_in_dim.20
  1.4 0.7 broadcast_in_dim.21
  2.1 0.8 copy.36
  2.9 0.3 compare_reduce_fusion
  3.2 0.6 convert_element_type.25.chosen_ref
  3.8 0.8 copy.35
  4.6 0.9 constant_dynamic-slice_fusion
  5.6 0.8 maximum_maximum_fusion.wout_shard
  6.3 1.1 constant_dynamic-slice_fusion.3
  7.4 1.1 constant_dynamic-slice_fusion.1
  8.5 0.9 concatenate.6.win_shard
  9.5 3.1 negate_select_fusion
  12.5 126.6 %front.1 = (bf16[16,128,1536]{2,1,0:T(8,128)(2,1)}, bf16[1536,384]{1,0:T(8,128)(2,1)}, bf16[208,1536]{1,0:T(8,128)(2,1)}, bf16[1024,1536]{1,0:T(8,128)(2,1)}, bf...) custom-call(bf16[128,1536]{1,0:T(8,128)(2,1)} %bitcast.15, ...), custom_call_target="tpu_custom_call" | custom-call | flops 8000000000 | bytes 150000000 | tf_op jit(solution)/shard_map/front/pallas_call | solution.py:984
  139.1 140.0 %experts_back.1 = (bf16[2048,1536]{1,0:T(8,128)(2,1)}, bf16[8,128,1536]{2,1,0:T(8,128)(2,1)}, bf16[8,128,128]{2,1,0:T(8,128)(2,1)}, f32[128,1536]{1,0:T(8,128)},...) custom-call(bf16[2048,1536]{1,0:T(8,128)(2,1)} %bitcast.21, ...), custom_call_target="tpu_custom_call" | custom-call | flops 43000000512 | bytes 42000000 | tf_op jit(solution)/shard_map/experts_back/pallas_call | solution.py:1720
  279.1 50.3 %attend_back.1 = (bf16[1024,1536]{1,0:T(8,128)(2,1)}, bf16[1536,384]{1,0:T(8,128)(2,1)}, bf16[192,384]{1,0:T(8,128)(2,1)}, f32[128,1536]{1,0:T(8,128)}, bf16[128...) custom-call(bf16[1024,1536]{1,0:T(8,128)(2,1)} %bitcast.25, ...), custom_call_target="tpu_custom_call" | custom-call | flops 20000000000 | bytes 30000000 | tf_op jit(solution)/shard_map/attend_back/pallas_call | solution.py:1207
  329.4 72.3 %close_transfers.1 = (bf16[128,1536]{1,0:T(8,128)(2,1)}, bf16[128,1536]{1,0:T(8,128)(2,1)}, bf16[8,384,384]{2,1,0:T(8,128)(2,1)}, bf16[8,192,384]{2,1,0:T(8,128)...) custom-call(bf16[8,128,1536]{2,1,0:T(8,128)(2,1)} %bitcast.13, f32[128,1536]{1,0:T(8,128)} %get-tuple-element.88.e_own, ...), custom_call_target="tpu_custom_call" | custom-call | bytes 200000000 | tf_op jit(solution)/shard_map/close_transfers/pallas_call | solution.py:748
  401.6 0.8 convert_reduce_fusion
  402.5 0.6 slice_reduce_fusion
  403.1 0.9 reduce_sum.19
  403.9 0.6 fusion.8
  404.5 0.0 copy-start.1
  404.6 0.0 copy-start
  404.6 9.0 %finish.1 = (f32[384,1536]{1,0:T(8,128)}, f32[384,512]{1,0:T(8,128)}, f32[384,512]{1,0:T(8,128)}, f32[384,24]{1,0:T(8,128)}, f32[1536,384]{1,0:T(8,128)}, /*inde...) custom-call(bf16[8,384,384]{2,1,0:T(8,128)(2,1)} %get-tuple-element.97.in_ref, ...), custom_call_target="tpu_custom_call" | custom-call | bytes 25000000 | tf_op jit(solution)/shard_map/finish/pallas_call | solution.py:1836
  413.6 1.6 copy.37
  415.2 0.0 copy-done.1
  415.2 0.7 copy.40
  416.0 0.0 copy-done
  416.0 0.7 copy.41
  (6 shorter events, 0.0 us)
Async XLA Ops:
  404.5 10.7 %copy-start.1 = (bf16[128,1536]{1,0:T(8,128)(2,1)S(1)}, bf16[128,1536]{1,0:T(8,128)(2,1)}, u32[]{:S(2)}) copy-start(bf16[128,1536]{1,0:T(8,128)(2,1)} %get-tuple-element.94) | copy-start | bytes 1179652
  404.6 11.4 %copy-start = (bf16[128,1536]{1,0:T(8,128)(2,1)S(1)}, bf16[128,1536]{1,0:T(8,128)(2,1)}, u32[]{:S(2)}) copy-start(bf16[128,1536]{1,0:T(8,128)(2,1)} %get-tuple-element.95) | copy-start | bytes 1179652
